TPU v7x, 32 devices: a whole 2x2x4 slice. The times are simulated.
32 devices in a mesh: section: 4 (over y, x), replica: 8 (over z, core).
Axes of the slice: x: 2, y: 2, z: 4, core: 2. Of those that a mesh axis runs over, the one named last changes fastest.
Arguments:
- hidden: bfloat16 [4, 2048, 64], P('section', 'replica'), may hold values from -6 to 6
- out_grad: bfloat16 [4, 2048, 6144], P('section', 'replica'), may hold values from -6 to 6
- weights_old: bfloat16 [256, 6144], P('section'), may hold values from -6 to 6
- master: float32 [256, 6144], P(('section', 'replica')), may hold values from -6 to 6
- first_moment: float32 [256, 6144], P(('section', 'replica')), may hold values from -4 to 4
- second_moment: float32 [256, 6144], P(('section', 'replica')), may hold values from 0.01 to 1
- owner_order: int32 [8], replicated, may hold values from 0 to 7, each once
- step_count: int32 [1], replicated, may hold values from 1 to 8
Outputs:
- new_master: float32 [256, 6144], P(('section', 'replica'))
- new_first: float32 [256, 6144], P(('section', 'replica'))
- new_second: float32 [256, 6144], P(('section', 'replica'))
- checkpoint: float32 [3, 256, 6144], P(None, ('section', 'replica'))
- weights_new: bfloat16 [256, 6144], P('section')
- hidden_grad: bfloat16 [4, 2048, 64], P('section', 'replica')
Inputs may be any that keep to these rules, and one draw needn't show every extreme that they name: Replica r owns block owner_order[r] of its section's bucket.
All inputs are finite; a program needn't handle non-finite values.
Results may differ from a plain program's by a relative error of at most 0.005.
Values may be sent and summed in bfloat16 or wider, within the bound.
No kernel may reach another device: no remote copies, remote signals or barrier semaphores. Data moves between devices by JAX's collectives and lax.ppermute only.
A program may use at most 64 MiB of HBM per device.

v0:
```python
import jax
import jax.numpy as jnp
from jax import lax
from jax.sharding import PartitionSpec as P


def passed_along(array, axis, by):
    devices = lax.axis_size(axis)
    return lax.ppermute(array, axis, [(i, (i + by) % devices) for i in range(devices)])


def adam_update(grads, master, first, second, steps):
    first_new = 0.9 * first + 0.1 * grads
    second_new = 0.95 * second + 0.05 * grads * grads
    fix_one = 1.0 - jnp.power(0.9, steps)
    fix_two = 1.0 - jnp.power(0.95, steps)
    update = first_new / fix_one / (jnp.sqrt(second_new / fix_two) + 1e-08)
    master_new = master - 0.05 * (update + 0.1 * master)
    return (master_new, first_new, second_new)


def per_device(
    hidden, out_grad, weights_old, master, first_moment, second_moment, owner_order, step_count
):
    replicas = lax.axis_size("replica")
    block = master.shape[0]
    slab_rows = weights_old.shape[0]
    width = out_grad.shape[2]
    acts = hidden[0]
    grads_out = out_grad[0]
    tokens = acts.shape[0]
    acts_blocks = acts.reshape(tokens, replicas, block)
    steps = step_count[0].astype(jnp.float32)
    columns = jnp.take(acts_blocks, owner_order, axis=1).reshape(tokens, slab_rows)
    product = lax.dot_general(
        columns, grads_out, (((0,), (0,)), ((), ())), preferred_element_type=jnp.float32
    )
    full_term = product / tokens
    owned = lax.psum_scatter(full_term, "replica", scatter_dimension=0, tiled=True)
    back = lax.dot_general(
        grads_out, weights_old, (((1,), (1,)), ((), ())), preferred_element_type=jnp.float32
    )
    hidden_grad = (back * width ** (-0.5)).astype(jnp.bfloat16)
    new_master, new_first, new_second = adam_update(
        owned, master, first_moment, second_moment, steps
    )
    moved = passed_along((new_master, new_first, new_second), "replica", 1)
    checkpoint = jnp.stack([moved[0], moved[1], moved[2]])
    gathered = lax.all_gather(new_master.astype(jnp.bfloat16), "replica", axis=0, tiled=True)
    inverse = (
        jnp.zeros((replicas,), jnp.int32).at[owner_order].set(jnp.arange(replicas, dtype=jnp.int32))
    )
    weights_new = jnp.take(gathered.reshape(replicas, block, width), inverse, axis=0).reshape(
        slab_rows, width
    )
    return (new_master, new_first, new_second, checkpoint, weights_new, hidden_grad[None])


def solution(mesh):
    placed = (
        P("section", "replica", None),
        P("section", "replica", None),
        P("section", None),
        P(("section", "replica"), None),
        P(("section", "replica"), None),
        P(("section", "replica"), None),
        P(),
        P(),
    )
    return jax.shard_map(
        per_device,
        mesh=mesh,
        in_specs=placed,
        out_specs=(
            P(("section", "replica"), None),
            P(("section", "replica"), None),
            P(("section", "replica"), None),
            P(None, ("section", "replica"), None),
            P("section", None),
            P("section", "replica", None),
        ),
        check_vma=False,
    )
```

profile of v0, /device:TPU:0, one launch (start us, length us, event | category | flops | bytes accessed | tf_op | source)
XLA Modules:
  0.0 86.1 jit_solution(4260345061217673802)
XLA Ops:
  7.2 0.0 copy-start
  7.2 0.0 reduce-scatter.2.cloned.1.call-start
  7.2 0.8 compare_select_fusion.1
  8.0 0.8 compare_and_fusion.1
  8.8 1.3 %gather_fusion = bf16[8,256,8]{1,2,0:T(8,128)(2,1)S(1)} fusion(bf16[256,8,8]{0,2,1:T(8,128)(2,1)} %bitcast.28, s32[1024]{0:T(1024)S(1)} %pad_clamp_fusion.1), kind=kCustom, calls=%fused_computation | custom fusion | bytes 65568 | tf_op jit(solution)/shard_map/jit(_take)/gather | solution.py:34
  10.1 0.0 copy-done
  10.1 1.9 %convolution_multiply_fusion = f32[64,6144]{1,0:T(8,128)} fusion(bf16[1,256,6144]{2,1,0:T(8,128)(2,1)S(1)} %copy-done, bf16[8,256,8]{1,2,0:T(8,128)(2,1)S(1)} %gather_fusion, pred[8]{0:T(512)(128)(4,1)S(1)} %compare_and_fusion.1), kind=kOutput, calls=%fused_computation.3 | convolution fusion | flops 201736192 | bytes 4751368 | tf_op jit(solution)/shard_map/dot_general | solution.py:35
  12.0 0.0 copy-start.1
  12.0 0.0 copy-start.2
  12.0 0.0 reduce-scatter.2.cloned.1.call-update
  12.8 0.6 scatter_custom_fusion
  13.4 0.1 broadcast_in_dim.35
  13.5 0.1 broadcast_in_dim.36
  13.6 2.8 %fusion.9 = bf16[1,256,64]{1,2,0:T(8,128)(2,1)} fusion(bf16[64,6144]{1,0:T(8,128)(2,1)} %param.10, bf16[1,256,6144]{2,1,0:T(8,128)(2,1)S(1)} %copy-done), kind=kOutput, calls=%fused_computation.9 | convolution fusion | flops 201359360 | bytes 3964928 | tf_op jit(solution)/shard_map/dot_general | solution.py:40
  16.5 32.6 %reduce-scatter.2.cloned.1.call-done = f32[8,6144]{1,0:T(8,128)} async-done(((f32[64,6144]{1,0:T(8,128)}), f32[8,6144]{1,0:T(8,128)}) %reduce-scatter.2.cloned.1.call-update) | async-done | bytes 196624 | tf_op jit(solution)/shard_map/reduce_scatter | solution.py:39
  49.0 0.0 copy-done.1
  49.0 0.0 copy-done.2
  49.0 1.9 %fusion.20 = (bf16[8,6144]{1,0:T(8,128)(2,1)S(1)}, f32[8,6144]{1,0:T(8,128)}, f32[8,6144]{1,0:T(8,128)}, f32[8,6144]{1,0:T(8,128)}) fusion(f32[8,6144]{1,0:T(8,128)S(1)} %copy-done.1, f32[]{:T(128)} %bitcast.5, f32[]{:T(128)} %bitcast.4, f32[8,6144]{1,0:T(8,128)} %reduce-scatter.2.cloned.1.call-done, f32[8,6144]{1,0:T(8,128)S(1)} %copy-done.2, ...), kind=kLoop, calls=%fused_computation.29 | loop fusion | flops 786432 | bytes 1474568 | tf_op jit(solution)/shard_map/convert_element_type | solution.py:49
  50.9 0.0 collective-permute-start
  51.0 0.0 collective-permute-start.1
  51.0 0.1 collective-permute-start.2
  51.0 21.7 %all_gather.3 = bf16[64,6144]{1,0:T(8,128)(2,1)} all-gather(bf16[8,6144]{1,0:T(8,128)(2,1)S(1)} %get-tuple-element.6), channel_id=1, replica_groups=mesh['section'=4,'replica'=8] {'replica'}, dimensions={0}, use_global_device_ids=true | all-gather | bytes 884736 | tf_op jit(solution)/shard_map/all_gather | solution.py:49
  72.7 2.6 %gather_fusion.1 = bf16[8,8,6144]{2,1,0:T(8,128)(2,1)} fusion(bf16[8,8,6144]{2,1,0:T(8,128)(2,1)} %bitcast.29, s32[1024]{0:T(1024)S(1)} %pad_clamp_fusion), kind=kCustom, calls=%fused_computation.1 | custom fusion | bytes 1572896 | tf_op jit(solution)/shard_map/jit(_take)/gather | solution.py:53
  75.3 2.2 %bitcast_select_fusion = bf16[64,6144]{1,0:T(8,128)(2,1)} fusion(bf16[8,8,6144]{2,1,0:T(8,128)(2,1)} %gather_fusion.1, pred[64]{0:T(512)(128)(4,1)S(1)} %broadcast_in_dim.36), kind=kLoop, calls=%fused_computation.10 | loop fusion | flops 393216 | bytes 1572928 | tf_op jit(solution)/shard_map/jit(_take)/select_n | solution.py:53
  77.5 0.0 collective-permute-done
  77.5 0.0 collective-permute-done.1
  77.5 0.0 collective-permute-done.2
  77.5 1.8 %pad_maximum_fusion = f32[3,8,6144]{2,1,0:T(8,128)} fusion(f32[1,8,6144]{2,1,0:T(8,128)} %bitcast.8, f32[1,8,6144]{2,1,0:T(8,128)S(1)} %bitcast.31, f32[1,8,6144]{2,1,0:T(8,128)S(1)} %bitcast.30), kind=kLoop, calls=%fused_computation.11 | loop fusion | flops 294912 | bytes 1179648 | tf_op jit(solution)/shard_map/stack | solution.py:48
  (5 shorter events, 0.0 us)
Async XLA Ops:
  7.2 3.0 %copy-start = (bf16[1,256,6144]{2,1,0:T(8,128)(2,1)S(1)}, bf16[1,256,6144]{2,1,0:T(8,128)(2,1)}, u32[]{:S(2)}) copy-start(bf16[1,256,6144]{2,1,0:T(8,128)(2,1)} %param.9) | copy-start | bytes 9437188
  7.2 41.9 %reduce-scatter.2.cloned.1.call-start = ((), (), s32[]{:S(2)}) async-start(), calls=%async_computation.1 | async-start | bytes 1769472 | tf_op jit(solution)/shard_map/reduce_scatter | solution.py:39
  12.0 37.0 %copy-start.1 = (f32[8,6144]{1,0:T(8,128)S(1)}, f32[8,6144]{1,0:T(8,128)}, u32[]{:S(2)}) copy-start(f32[8,6144]{1,0:T(8,128)} %param.11) | copy-start | bytes 589828
  12.0 37.0 %copy-start.2 = (f32[8,6144]{1,0:T(8,128)S(1)}, f32[8,6144]{1,0:T(8,128)}, u32[]{:S(2)}) copy-start(f32[8,6144]{1,0:T(8,128)} %param.13) | copy-start | bytes 589828
  50.9 26.5 %collective-permute-start = (f32[8,6144]{1,0:T(8,128)}, f32[8,6144]{1,0:T(8,128)S(1)}, u32[]{:S(2)}, u32[]{:S(2)}) collective-permute-start(f32[8,6144]{1,0:T(8,128)} %get-tuple-element.7), channel_id=1, source_target_pairs={{0,1},{1,2},{2,3},{3,4},{4,5},{5,6},{6,7},{7,0},{8,9},{9,10},{10,1... | collective-permute-start | bytes 589832 | tf_op jit(solution)/shard_map/ppermute | solution.py:9
  51.0 26.5 %collective-permute-start.1 = (f32[8,6144]{1,0:T(8,128)}, f32[8,6144]{1,0:T(8,128)S(1)}, u32[]{:S(2)}, u32[]{:S(2)}) collective-permute-start(f32[8,6144]{1,0:T(8,128)} %get-tuple-element.9), channel_id=1, source_target_pairs={{0,1},{1,2},{2,3},{3,4},{4,5},{5,6},{6,7},{7,0},{8,9},{9,10},{10,1... | collective-permute-start | bytes 589832 | tf_op jit(solution)/shard_map/ppermute | solution.py:9
  51.0 26.5 %collective-permute-start.2 = (f32[8,6144]{1,0:T(8,128)}, f32[8,6144]{1,0:T(8,128)}, u32[]{:S(2)}, u32[]{:S(2)}) collective-permute-start(f32[8,6144]{1,0:T(8,128)} %get-tuple-element.8), channel_id=1, source_target_pairs={{0,1},{1,2},{2,3},{3,4},{4,5},{5,6},{6,7},{7,0},{8,9},{9,10},{10,1... | collective-permute-start | bytes 589832 | tf_op jit(solution)/shard_map/ppermute | solution.py:9
Sparse Core Ops, SparseCore 0:
  12.2 36.8 reduce-scatter.1
where the time goes:
time: 86.5 us; the launch traced here: 86.1 us
  waiting for transfers between devices  32.6 us (38%)
  blocking collectives  21.7 us (25%)
  between operations  14.9 us (17%)
  other arithmetic  7.43 us (9%)
  local copies, waits for them, and re-layouts  4.71 us (5%)
  matrix products  4.71 us (5%)
    reduce_scatter x1, waiting for transfers between devices, per_device(): lax.psum_scatter(full_term, 'replica', scatter_dimension=0, tiled=True)  32.6 us
    all_gather x1, blocking collectives, per_device(): lax.all_gather(new_master.astype(jnp.bfloat16), 'replica', axis=0, tiled=...  21.7 us
    dot_general x1, matrix products, per_device(): lax.dot_general(grads_out, weights_old, (((1,), (1,)), ((), ())), preferr...  2.83 us
    gather x1, local copies, waits for them, and re-layouts, per_device(): jnp.take(gathered.reshape(replicas, block, width), inverse, axis=0)  2.62 us
    select_n x2, other arithmetic, per_device(): jnp.take(gathered.reshape(replicas, block, width), inverse, axis=0)  2.15 us
    convert_element_type x1, other arithmetic, per_device(): new_master.astype(jnp.bfloat16)  1.9 us
    dot_general x1, matrix products, per_device(): lax.dot_general(columns, grads_out, (((0,), (0,)), ((), ())), preferred_e...  1.87 us
    another operation x1, other arithmetic, per_device(): checkpoint = jnp.stack([moved[0], moved[1], moved[2]])  1.78 us
  transfers between devices with their start and end apart: 4, of which 1 were waited for; matrix products, arithmetic and copies ran while one was open for 10% of the time, Pallas kernels for 0%

commit v1 on v0

v1 whole, which is shorter than its diff:
```python
import functools

import jax
import jax.numpy as jnp
from jax import lax
from jax.experimental import pallas as pl
from jax.experimental.pallas import tpu as pltpu
from jax.sharding import PartitionSpec as P


def passed_along(array, axis, by):
    devices = lax.axis_size(axis)
    return lax.ppermute(array, axis, [(i, (i + by) % devices) for i in range(devices)])


def adam_update(grads, master, first, second, fix_one, fix_two):
    first_new = 0.9 * first + 0.1 * grads
    second_new = 0.95 * second + 0.05 * grads * grads
    update = first_new / fix_one / (jnp.sqrt(second_new / fix_two) + 1e-08)
    master_new = master - 0.05 * (update + 0.1 * master)
    return (master_new, first_new, second_new)


def plain_device(
    hidden, out_grad, weights_old, master, first_moment, second_moment, owner_order, step_count
):
    replicas = lax.axis_size("replica")
    block = master.shape[0]
    slab_rows = weights_old.shape[0]
    width = out_grad.shape[2]
    acts = hidden[0]
    grads_out = out_grad[0]
    tokens = acts.shape[0]
    acts_blocks = acts.reshape(tokens, replicas, block)
    steps = step_count[0].astype(jnp.float32)
    columns = jnp.take(acts_blocks, owner_order, axis=1).reshape(tokens, slab_rows)
    product = lax.dot_general(
        columns, grads_out, (((0,), (0,)), ((), ())), preferred_element_type=jnp.float32
    )
    owned = lax.psum_scatter(product / tokens, "replica", scatter_dimension=0, tiled=True)
    back = lax.dot_general(
        grads_out, weights_old, (((1,), (1,)), ((), ())), preferred_element_type=jnp.float32
    )
    hidden_grad = (back * width ** (-0.5)).astype(jnp.bfloat16)
    fix_one = 1.0 - jnp.power(0.9, steps)
    fix_two = 1.0 - jnp.power(0.95, steps)
    updated = adam_update(owned, master, first_moment, second_moment, fix_one, fix_two)
    checkpoint = jnp.stack(passed_along(updated, "replica", 1))
    gathered = lax.all_gather(updated[0].astype(jnp.bfloat16), "replica", axis=0, tiled=True)
    inverse = (
        jnp.zeros((replicas,), jnp.int32).at[owner_order].set(jnp.arange(replicas, dtype=jnp.int32))
    )
    weights_new = jnp.take(gathered.reshape(replicas, block, width), inverse, axis=0).reshape(
        slab_rows, width
    )
    return (*updated, checkpoint, weights_new, hidden_grad[None])


SMEM = functools.partial(pl.BlockSpec, memory_space=pltpu.SMEM)
VMEM = functools.partial(pl.BlockSpec, memory_space=pltpu.VMEM)
HBM = functools.partial(pl.BlockSpec, memory_space=pltpu.HBM)


def params():
    return pltpu.CompilerParams(vmem_limit_bytes=8 << 20)


def cost(flops, moved):
    return pl.CostEstimate(flops=flops, bytes_accessed=moved, transcendentals=0)


def in_hbm(*arrays):
    return tuple(pltpu.with_memory_space_constraint(x, pltpu.HBM) for x in arrays)


def this_core():
    return lax.axis_index("replica") % 2


def distances_of(chips, core):
    ks = sorted(range(1, chips), key=lambda k: (k ^ (chips >> 1), k))
    return [0] + (ks[-1:] + ks[:-1] if core else ks)


def distance_at(place, chips, core):
    first, second = (distances_of(chips, c)[place] for c in range(2))
    return jnp.where(core == 0, first, second)


def send_kernel(
    order_hbm, acts_hbm, grads_hbm, first_hbm, second_hbm,
    send_ref, grads, picked, first, second, moments, order, acts, sems,
):
    replicas = order.shape[0]
    rows, tokens = acts.shape
    block, half = rows // replicas, rows // 2
    steps = sems.shape[0] - 4
    tile = grads.shape[1] // steps
    small = [
        pltpu.make_async_copy(order_hbm, order, sems.at[steps]),
        pltpu.make_async_copy(acts_hbm, acts, sems.at[steps + 1]),
    ]
    spans = [pl.ds(step * tile, tile) for step in range(steps)]
    tiles = [
        pltpu.make_async_copy(grads_hbm.at[:, span], grads.at[:, span], sems.at[step])
        for step, span in enumerate(spans)
    ]
    states = [
        pltpu.make_async_copy(first_hbm, first, sems.at[steps + 2]),
        pltpu.make_async_copy(second_hbm, second, sems.at[steps + 3]),
    ]
    for copy in small + tiles + states:
        copy.start()
    me = lax.axis_index("replica")
    chip, core = me // 2, me % 2
    at = lax.broadcasted_iota(jnp.int32, (rows, rows), 0)
    column = lax.broadcasted_iota(jnp.int32, (rows, rows), 1)
    source = at
    for copy in small:
        copy.wait()
    for place in range(replicas):
        at_place, mine = place % (replicas // 2), place // (replicas // 2)
        lane = core if mine else 1 - core
        owner = 2 * (chip ^ distance_at(at_place, replicas // 2, lane)) + lane
        inside = (at >= place * block) & (at < (place + 1) * block)
        source = jnp.where(inside, at + (order[owner] - place) * block, source)
    chosen = jnp.where(column == source, 1.0, 0.0).astype(acts.dtype)
    both = jnp.dot(chosen, acts[...], preferred_element_type=jnp.float32).astype(picked.dtype)
    picked[...] = both[half:]
    mine = both[:half]
    for copy, span in zip(tiles, spans):
        copy.wait()
        product = jnp.dot(mine, grads[:, span], preferred_element_type=jnp.float32)
        send_ref[:, span] = (product * (1.0 / tokens)).astype(send_ref.dtype)
    for at, (copy, state) in enumerate(zip(states, (first, second))):
        copy.wait()
        moments[at * block : (at + 1) * block] = state[...].astype(moments.dtype)


def slab_to_send(order, acts_t, grads_out, first, second, steps):
    rows, tokens = acts_t.shape
    block = first.shape[0]
    width = grads_out.shape[1]
    return pl.pallas_call(
        send_kernel,
        in_specs=[HBM()] * 5,
        out_specs=[VMEM()] * 6,
        out_shape=[
            jax.ShapeDtypeStruct((rows // 2, width), jnp.bfloat16),
            jax.ShapeDtypeStruct((tokens, width), grads_out.dtype),
            jax.ShapeDtypeStruct((rows // 2, tokens), acts_t.dtype),
            jax.ShapeDtypeStruct((block, width), jnp.float32),
            jax.ShapeDtypeStruct((block, width), jnp.float32),
            jax.ShapeDtypeStruct((2 * block, width), jnp.bfloat16),
        ],
        scratch_shapes=[
            pltpu.SMEM(order.shape, order.dtype),
            pltpu.VMEM((rows, tokens), acts_t.dtype),
            pltpu.SemaphoreType.DMA((steps + 4,)),
        ],
        compiler_params=params(),
        cost_estimate=cost(rows * tokens * width, 2 * tokens * width),
        name="slab_to_send",
    )(*in_hbm(order, acts_t, grads_out, first, second))


def keep_kernel(picked, grads, master_hbm, keep_ref, master, sem):
    copy = pltpu.make_async_copy(master_hbm, master, sem)
    copy.start()
    tokens = grads.shape[0]
    tile = grads.shape[1] // 4
    for step in range(4):
        span = pl.ds(step * tile, tile)
        product = jnp.dot(picked[...], grads[:, span], preferred_element_type=jnp.float32)
        keep_ref[:, span] = product * (1.0 / tokens)
    copy.wait()


def slab_to_keep(picked, grads, master):
    rows, tokens = picked.shape
    width = master.shape[1]
    return pl.pallas_call(
        keep_kernel,
        in_specs=[VMEM()] * 2 + [HBM()],
        out_specs=[VMEM()] * 2,
        out_shape=[
            jax.ShapeDtypeStruct((rows, width), jnp.float32),
            jax.ShapeDtypeStruct(master.shape, jnp.float32),
        ],
        scratch_shapes=[pltpu.SemaphoreType.DMA],
        compiler_params=params(),
        cost_estimate=cost(2 * rows * tokens * width, 2 * tokens * width),
        name="slab_to_keep",
    )(picked, grads, *in_hbm(master))


def back_kernel(scale, core, weights_hbm, grads, *refs):
    out, weights, result, sems, sem = refs[-5:]
    steps = sems.shape[0]
    tile = grads.shape[1] // steps

    @pl.when(this_core() == core)
    def _():
        spans = [pl.ds(step * tile, tile) for step in range(steps)]
        copies = [
            pltpu.make_async_copy(weights_hbm.at[:, span], weights.at[:, span], sems.at[step])
            for step, span in enumerate(spans)
        ]
        for copy in copies:
            copy.start()
        total = None
        for copy, span in zip(copies, spans):
            copy.wait()
            term = lax.dot_general(
                weights[:, span], grads[:, span], (((1,), (1,)), ((), ())),
                preferred_element_type=jnp.float32,
            )
            total = term if total is None else total + term
        result[...] = (total * scale).astype(result.dtype)
        copy = pltpu.make_async_copy(result, out, sem)
        copy.start()
        copy.wait()


def hidden_gradient(weights_old, grads, core, steps, earlier=()):
    rows, width = weights_old.shape
    tokens = grads.shape[0]
    return pl.pallas_call(
        functools.partial(back_kernel, width ** (-0.5), core),
        in_specs=[HBM(), VMEM()] + [HBM()] * len(earlier),
        out_specs=HBM(),
        out_shape=jax.ShapeDtypeStruct((rows, tokens), jnp.bfloat16),
        input_output_aliases={2 + at: at for at in range(len(earlier))},
        scratch_shapes=[
            pltpu.VMEM((rows, width), weights_old.dtype),
            pltpu.VMEM((rows, tokens), jnp.bfloat16),
            pltpu.SemaphoreType.DMA((steps,)),
            pltpu.SemaphoreType.DMA,
        ],
        compiler_params=params(),
        cost_estimate=cost(2 * rows * tokens * width, 2 * (tokens + rows) * width),
        name="hidden_gradient",
    )(*in_hbm(weights_old), grads, *earlier)


def pair_kernel(keep_ref, got_ref, own_ref, *send_refs):
    block = own_ref.shape[0]
    own_ref[...] = keep_ref[:block] + got_ref[:block].astype(jnp.float32)
    for away, send in enumerate(send_refs, 1):
        rows = slice(away * block, (away + 1) * block)
        send[...] = (keep_ref[rows] + got_ref[rows].astype(jnp.float32)).astype(send.dtype)


def pair_sum(keep, got, block):
    rows, width = keep.shape
    others = rows // block - 1
    return pl.pallas_call(
        pair_kernel,
        in_specs=[VMEM(), VMEM()],
        out_specs=[VMEM()] * (1 + others),
        out_shape=[jax.ShapeDtypeStruct((block, width), jnp.float32)]
        + [jax.ShapeDtypeStruct((block, width), jnp.bfloat16)] * others,
        compiler_params=params(),
        cost_estimate=cost(rows * width, 8 * rows * width),
        name="pair_sum",
    )(keep, got)


def update_kernel(fix_ref, *refs):
    parts, (master, first, second, grads_ref, send_master, send_grads) = refs[:-6], refs[-6:]
    grads = parts[0][...]
    for part in parts[1:]:
        grads = grads + part[...].astype(jnp.float32)
    grads_ref[...] = grads
    send_grads[...] = grads.astype(send_grads.dtype)
    new_master, _, _ = adam_update(
        grads, master[...], first[...], second[...], fix_ref[0:1, 0:1], fix_ref[1:2, 0:1]
    )
    send_master[...] = new_master.astype(send_master.dtype)


def update(fix, parts, states):
    block, width = parts[0].shape
    return pl.pallas_call(
        update_kernel,
        in_specs=[VMEM()] * (4 + len(parts)),
        out_specs=[VMEM()] * 3,
        out_shape=[
            jax.ShapeDtypeStruct((block, width), jnp.float32),
            jax.ShapeDtypeStruct((block, width), jnp.bfloat16),
            jax.ShapeDtypeStruct((block, width), jnp.bfloat16),
        ],
        compiler_params=params(),
        cost_estimate=cost(20 * block * width, 24 * block * width),
        name="update",
    )(fix, *parts, *states)


def states_kernel(fix_ref, master, first, second, grads, *outs):
    updated = adam_update(
        grads[...], master[...], first[...], second[...], fix_ref[0:1, 0:1], fix_ref[1:2, 0:1]
    )
    for out, value in zip(outs, updated):
        out[...] = value


def new_states(fix, states, grads):
    shape = states[0].shape
    return pl.pallas_call(
        states_kernel,
        in_specs=[VMEM()] * 5,
        out_specs=[VMEM()] * 3,
        out_shape=[jax.ShapeDtypeStruct(shape, jnp.float32)] * 3,
        compiler_params=params(),
        cost_estimate=cost(20 * states[0].size, 28 * states[0].size),
        name="new_states",
    )(fix, *states, grads)


def owner_at(place, chips, sibling):
    me = lax.axis_index("replica")
    lane = 1 - me % 2 if sibling else me % 2
    return 2 * (me // 2 ^ distance_at(place, chips, lane)) + lane


def place_kernel(chips, order, *refs):
    near, far = refs[:chips], refs[chips : 2 * chips]
    packed, moved, weights, checkpoint, partner, sems = refs[2 * chips :]
    block = moved.shape[0]
    replicas = order.shape[0]
    previous = lax.rem(lax.axis_index("replica") + replicas - 1, replicas)
    copies = []
    for sibling, pieces in enumerate((near, far)):
        for at, piece in enumerate(pieces):
            row = pl.multiple_of(order[owner_at(at, chips, sibling)] * block, block)
            target = weights.at[pl.ds(row, block), :]
            copies.append(pltpu.make_async_copy(piece, target, sems.at[len(copies)]))
    for copy in copies:
        copy.start()
    grads = moved[...].astype(jnp.float32)
    partner[1] = 0.9 * packed[:block].astype(jnp.float32) + 0.1 * grads
    partner[2] = 0.95 * packed[block:].astype(jnp.float32) + 0.05 * grads * grads
    for at, piece in enumerate(far):

        @pl.when(owner_at(at, chips, 1) == previous)
        def _():
            partner[0] = piece[...].astype(jnp.float32)

    last = pltpu.make_async_copy(partner, checkpoint, sems.at[replicas])
    last.start()
    for copy in copies:
        copy.wait()
    last.wait()


def place(order, near, far, packed, moved):
    block, width = moved.shape
    chips = len(near)
    rows = 2 * chips * block
    return pl.pallas_call(
        functools.partial(place_kernel, chips),
        in_specs=[SMEM()] + [VMEM()] * (2 * chips + 2),
        out_specs=[HBM()] * 2,
        out_shape=[
            jax.ShapeDtypeStruct((rows, width), jnp.bfloat16),
            jax.ShapeDtypeStruct((3, block, width), jnp.float32),
        ],
        scratch_shapes=[
            pltpu.VMEM((3, block, width), jnp.float32),
            pltpu.SemaphoreType.DMA((2 * chips + 1,)),
        ],
        compiler_params=params(),
        cost_estimate=cost(0, 8 * rows * width),
        name="place",
    )(order, *near, *far, packed, moved)


def tiled_device(
    hidden, out_grad, weights_old, master, first_moment, second_moment, owner_order, step_count
):
    replicas = lax.axis_size("replica")
    chips = replicas // 2
    block, _ = master.shape

    def permuted(piece, target):
        return lax.ppermute(piece, "replica", [(i, target(i)) for i in range(replicas)])

    def across(piece, at):
        ks = [distances_of(chips, core)[at] for core in range(2)]
        return permuted(piece, lambda i: i ^ (2 * ks[i % 2]))

    def to_sibling(piece):
        return permuted(piece, lambda i: i ^ 1)

    def along_ring(piece):
        return permuted(piece, lambda i: (i + 1) % replicas)

    steps = step_count[0].astype(jnp.float32)
    fix = jnp.stack([1.0 - jnp.power(0.9, steps), 1.0 - jnp.power(0.95, steps)])
    fix = jnp.broadcast_to(fix[:, None], (2, 128))

    send, grads_out, picked, first, second, packed = slab_to_send(
        owner_order, hidden[0].T, out_grad[0], first_moment, second_moment, 4
    )
    got = to_sibling(send)
    keep, loaded = slab_to_keep(picked, grads_out, master)
    states = (loaded, first, second)
    packed = along_ring(packed)
    own, *sends = pair_sum(keep, got, block)
    hidden_grad = hidden_gradient(weights_old, grads_out, 1, 2)
    hidden_grad = hidden_gradient(weights_old, grads_out, 0, 2, (hidden_grad,))
    parts = [own] + [across(sends[k - 1], k) for k in range(1, chips)]
    grads, send_master, send_grads = update(fix, parts, states)
    near = [send_master] + [across(send_master, k) for k in range(1, chips)]
    updated = new_states(fix, states, grads)
    moved = along_ring(send_grads)
    far = [to_sibling(piece) for piece in near]
    weights_new, checkpoint = place(owner_order, near, far, packed, moved)
    return (*updated, checkpoint, weights_new, hidden_grad.T[None])


def fits(replicas, block, width):
    chips = replicas // 2
    return block % 8 == 0 and width % 512 == 0 and replicas % 2 == 0 and chips & (chips - 1) == 0


def per_device(*arrays):
    block, width = arrays[3].shape
    if not fits(lax.axis_size("replica"), block, width):
        return plain_device(*arrays)
    return tiled_device(*arrays)


def solution(mesh):
    devices = P(("section", "replica"), None)
    return jax.shard_map(
        per_device,
        mesh=mesh,
        in_specs=(
            P("section", "replica", None),
            P("section", "replica", None),
            P("section", None),
            devices,
            devices,
            devices,
            P(),
            P(),
        ),
        out_specs=(
            devices,
            devices,
            devices,
            P(None, ("section", "replica"), None),
            P("section", None),
            P("section", "replica", None),
        ),
        check_vma=False,
    )
```

time: 86.5 us -> 38.4 us (0.44)
  waiting for transfers between devices: 32.6 us -> 10.5 us
  blocking collectives: 21.7 us -> 0 us
  starting transfers between devices: 0.1 us -> 17.1 us
  between operations: 14.9 us -> 1.47 us
  Pallas kernels: 0 us -> 9.03 us
  other arithmetic: 7.43 us -> 0.07 us
  matrix products: 4.71 us -> 0 us
  local copies, waits for them, and re-layouts: 4.71 us -> 0.08 us
    reduce_scatter x1 -> x0, waiting for transfers between devices: 32.6 us -> none  [per_device(): lax.psum_scatter(full_term, 'replica', scatter_dimension=0, tiled=True)]
    all_gather x1 -> x0, blocking collectives: 21.7 us -> none  [per_device(): lax.all_gather(new_master.astype(jnp.bfloat16), 'replica', axis=0, tiled=...]
    ppermute x3 -> x13, starting transfers between devices: 0.06 us -> 17.1 us  [permuted(): lax.ppermute(piece, 'replica', [(i, target(i)) for i in range(replicas)])]
    ppermute x3 -> x13, waiting for transfers between devices: 0.01 us -> 10.5 us  [permuted(): lax.ppermute(piece, 'replica', [(i, target(i)) for i in range(replicas)])]
    pallas_call x0 -> x8, Pallas kernels: none -> 9.03 us  [the longest x2 2.87 us: hidden_gradient(): pl.pallas_call(functools.partial(back_kernel, width ** (-0.5), core), in_...]
    dot_general x2 -> x0, matrix products: 4.71 us -> none  [the longest x1 2.83 us: per_device(): lax.dot_general(grads_out, weights_old, (((1,), (1,)), ((), ())), preferr...]
    gather x2 -> x0, local copies, waits for them, and re-layouts: 3.93 us -> none  [the longest x1 2.62 us: per_device(): jnp.take(gathered.reshape(replicas, block, width), inverse, axis=0)]
    select_n x3 -> x0, other arithmetic: 2.96 us -> none  [the longest x2 2.15 us: per_device(): jnp.take(gathered.reshape(replicas, block, width), inverse, axis=0)]
  transfers between devices with their start and end apart: 4 -> 13, of which waited for: 1 -> 4; matrix products, arithmetic and copies ran while one was open for 10% -> 0% of each run, Pallas kernels for 0% -> 13%
where the time goes in v1:
time: 38.4 us; the launch traced here: 38.2 us
  starting transfers between devices  17.1 us (45%)
  waiting for transfers between devices  10.5 us (27%)
  Pallas kernels  9.03 us (24%)
  between operations  1.47 us (4%)
    ppermute x13, starting transfers between devices, permuted(): lax.ppermute(piece, 'replica', [(i, target(i)) for i in range(replicas)])  17.1 us
    ppermute x13, waiting for transfers between devices, permuted(): lax.ppermute(piece, 'replica', [(i, target(i)) for i in range(replicas)])  10.5 us
    pallas_call x2, Pallas kernels, hidden_gradient(): pl.pallas_call(functools.partial(back_kernel, width ** (-0.5), core), in_...  2.87 us
    pallas_call x1, Pallas kernels, slab_to_send(): pl.pallas_call(send_kernel, in_specs=[HBM()] * 5, out_specs=[VMEM()] * 6,...  2.25 us
    pallas_call x1, Pallas kernels, place(): pl.pallas_call(functools.partial(place_kernel, chips), in_specs=[SMEM()]...  1.72 us
    pallas_call x1, Pallas kernels, slab_to_keep(): pl.pallas_call(keep_kernel, in_specs=[VMEM()] * 2 + [HBM()], out_specs=[V...  0.94 us
    pallas_call x1, Pallas kernels, new_states(): pl.pallas_call(states_kernel, in_specs=[VMEM()] * 5, out_specs=[VMEM()] *...  0.91 us
  transfers between devices with their start and end apart: 13, of which 4 were waited for; matrix products, arithmetic and copies ran while one was open for 0% of the time, Pallas kernels for 13%

profile of v1, /device:TPU:0, one launch (start us, length us, event | category | flops | bytes accessed | tf_op | source)
XLA Modules:
  0.0 38.2 jit_solution(6021594216779013580)
XLA Ops:
  0.6 2.2 %slab_to_send.1 = (bf16[32,6144]{1,0:T(8,128)(2,1)S(1)}, bf16[256,6144]{1,0:T(8,128)(2,1)S(1)}, bf16[32,256]{1,0:T(8,128)(2,1)S(1)}, f32[8,6144]{1,0:T(8,128)S(1...) custom-call(s32[8]{0:T(128)} %order.1, bf16[64,256]{1,0:T(8,128)(2,1)} %bitcast.9, bf16[256,6144]{1,0:T(8,128)(2,1)} %bitcast.7, ...), custom_call_target="tpu_custom_call" | custom-call | flops 100663296 | bytes 3145728 | tf_op jit(solution)/shard_map/slab_to_send/pallas_call | solution.py:144
  2.9 0.6 %collective-permute-start = (bf16[32,6144]{1,0:T(8,128)(2,1)S(1)}, bf16[32,6144]{1,0:T(8,128)(2,1)S(1)}, u32[]{:S(2)}, u32[]{:S(2)}) collective-permute-start(bf16[32,6144]{1,0:T(8,128)(2,1)S(1)} %get-tuple-element.32), channel_id=1, source_target_pairs={{0,1},{1,0},{2,3},{3,2},{4,5},{5,4},{6,7},{7,6},{8,9},{9,8},{10,11... | collective-permute-start | bytes 1179656 | tf_op jit(solution)/shard_map/ppermute | solution.py:386
  3.4 0.1 collective-permute-start.11
  4.2 0.9 %slab_to_keep.1 = (f32[32,6144]{1,0:T(8,128)S(1)}, f32[8,6144]{1,0:T(8,128)S(1)}) custom-call(bf16[32,256]{1,0:T(8,128)(2,1)S(1)} %get-tuple-element.26.picked, bf16[256,6144]{1,0:T(8,128)(2,1)S(1)} %get-tuple-element.27.grads, f32[8,6144]{1,0:T(8,128)} %master_hbm.1), custom_call_target="tpu_custom_call" | custom-call | flops 100663296 | bytes 3145728 | tf_op jit(solution)/shard_map/slab_to_keep/pallas_call | solution.py:182
  5.2 0.0 collective-permute-done.got_ref
  5.2 0.1 pair_sum.1
  5.3 4.1 %collective-permute-start.1 = (bf16[8,6144]{1,0:T(8,128)(2,1)S(1)}, bf16[8,6144]{1,0:T(8,128)(2,1)S(1)}, u32[]{:S(2)}, u32[]{:S(2)}) collective-permute-start(bf16[8,6144]{1,0:T(8,128)(2,1)S(1)} %get-tuple-element.34), channel_id=1, source_target_pairs={{0,4},{1,3},{2,6},{3,1},{4,0},{5,7},{6,2},{7,5},{8,12},{9,11},{10,... | collective-permute-start | bytes 294920 | tf_op jit(solution)/shard_map/ppermute | solution.py:386
  9.4 1.3 %collective-permute-start.2 = (bf16[8,6144]{1,0:T(8,128)(2,1)S(1)}, bf16[8,6144]{1,0:T(8,128)(2,1)S(1)}, u32[]{:S(2)}, u32[]{:S(2)}) collective-permute-start(bf16[8,6144]{1,0:T(8,128)(2,1)S(1)} %get-tuple-element.35), channel_id=1, source_target_pairs={{0,6},{1,5},{2,4},{3,7},{4,2},{5,1},{6,0},{7,3},{8,14},{9,13},{10,... | collective-permute-start | bytes 294920 | tf_op jit(solution)/shard_map/ppermute | solution.py:386
  10.7 0.2 collective-permute-start.3
  10.9 0.1 pad_maximum_fusion
  11.0 2.7 %collective-permute-done.1.refs_1_ = bf16[8,6144]{1,0:T(8,128)(2,1)S(1)} collective-permute-done((bf16[8,6144]{1,0:T(8,128)(2,1)S(1)}, bf16[8,6144]{1,0:T(8,128)(2,1)S(1)}, u32[]{:S(2)}, u32[]{:S(2)}) %collective-permute-start.1) | collective-permute-done | bytes 98336 | tf_op jit(solution)/shard_map/ppermute | solution.py:386
  13.7 3.1 %collective-permute-done.2.refs_2_ = bf16[8,6144]{1,0:T(8,128)(2,1)S(1)} collective-permute-done((bf16[8,6144]{1,0:T(8,128)(2,1)S(1)}, bf16[8,6144]{1,0:T(8,128)(2,1)S(1)}, u32[]{:S(2)}, u32[]{:S(2)}) %collective-permute-start.2) | collective-permute-done | bytes 98336 | tf_op jit(solution)/shard_map/ppermute | solution.py:386
  16.8 0.0 collective-permute-done.3.refs_3_
  16.8 0.1 broadcast_in_dim.4.fix_ref
  16.9 0.3 update.1
  17.2 3.4 %collective-permute-start.6 = (bf16[8,6144]{1,0:T(8,128)(2,1)S(1)}, bf16[8,6144]{1,0:T(8,128)(2,1)S(1)}, u32[]{:S(2)}, u32[]{:S(2)}) collective-permute-start(bf16[8,6144]{1,0:T(8,128)(2,1)S(1)} %get-tuple-element.41.refs_0_), channel_id=1, source_target_pairs={{0,2},{1,7},{2,0},{3,5},{4,6},{5,3},{6,4},{7,1},{8,10},{9,15},{10,... | collective-permute-start | bytes 294920 | tf_op jit(solution)/shard_map/ppermute | solution.py:386
  20.6 3.4 %collective-permute-start.5 = (bf16[8,6144]{1,0:T(8,128)(2,1)S(1)}, bf16[8,6144]{1,0:T(8,128)(2,1)S(1)}, u32[]{:S(2)}, u32[]{:S(2)}) collective-permute-start(bf16[8,6144]{1,0:T(8,128)(2,1)S(1)} %get-tuple-element.41.refs_0_), channel_id=1, source_target_pairs={{0,6},{1,5},{2,4},{3,7},{4,2},{5,1},{6,0},{7,3},{8,14},{9,13},{10,... | collective-permute-start | bytes 294920 | tf_op jit(solution)/shard_map/ppermute | solution.py:386
  24.0 0.0 collective-permute-start.4
  24.0 0.0 collective-permute-start.7
  24.0 0.0 collective-permute-done.11.refs_8_
  24.0 0.5 %collective-permute-start.12 = (bf16[8,6144]{1,0:T(8,128)(2,1)S(1)}, bf16[8,6144]{1,0:T(8,128)(2,1)S(1)}, u32[]{:S(2)}, u32[]{:S(2)}) collective-permute-start(bf16[8,6144]{1,0:T(8,128)(2,1)S(1)} %get-tuple-element.43), channel_id=1, source_target_pairs={{0,1},{1,2},{2,3},{3,4},{4,5},{5,6},{6,7},{7,0},{8,9},{9,10},{10,1... | collective-permute-start | bytes 294920 | tf_op jit(solution)/shard_map/ppermute | solution.py:386
  24.5 0.0 collective-permute-done.6.refs_3_
  24.5 0.6 %collective-permute-start.10 = (bf16[8,6144]{1,0:T(8,128)(2,1)S(1)}, bf16[8,6144]{1,0:T(8,128)(2,1)S(1)}, u32[]{:S(2)}, u32[]{:S(2)}) collective-permute-start(bf16[8,6144]{1,0:T(8,128)(2,1)S(1)} %collective-permute-done.6.refs_3_), channel_id=1, source_target_pairs={{0,1},{1,0},{2,3},{3,2},{4,5},{5,4},{6,7},{7,6},{8,9},{9,8},{10,11... | collective-permute-start | bytes 294920 | tf_op jit(solution)/shard_map/ppermute | solution.py:386
  25.2 4.3 %collective-permute-done.5.refs_2_ = bf16[8,6144]{1,0:T(8,128)(2,1)S(1)} collective-permute-done((bf16[8,6144]{1,0:T(8,128)(2,1)S(1)}, bf16[8,6144]{1,0:T(8,128)(2,1)S(1)}, u32[]{:S(2)}, u32[]{:S(2)}) %collective-permute-start.5) | collective-permute-done | bytes 98336 | tf_op jit(solution)/shard_map/ppermute | solution.py:386
  29.4 2.8 %collective-permute-start.9 = (bf16[8,6144]{1,0:T(8,128)(2,1)S(1)}, bf16[8,6144]{1,0:T(8,128)(2,1)S(1)}, u32[]{:S(2)}, u32[]{:S(2)}) collective-permute-start(bf16[8,6144]{1,0:T(8,128)(2,1)S(1)} %collective-permute-done.5.refs_2_), channel_id=1, source_target_pairs={{0,1},{1,0},{2,3},{3,2},{4,5},{5,4},{6,7},{7,6},{8,9},{9,8},{10,11... | collective-permute-start | bytes 294920 | tf_op jit(solution)/shard_map/ppermute | solution.py:386
  32.3 0.4 %collective-permute-done.4.refs_1_ = bf16[8,6144]{1,0:T(8,128)(2,1)S(1)} collective-permute-done((bf16[8,6144]{1,0:T(8,128)(2,1)S(1)}, bf16[8,6144]{1,0:T(8,128)(2,1)S(1)}, u32[]{:S(2)}, u32[]{:S(2)}) %collective-permute-start.4) | collective-permute-done | bytes 98336 | tf_op jit(solution)/shard_map/ppermute | solution.py:386
  32.7 0.0 collective-permute-start.8
  32.7 0.0 copy-start
  32.7 2.8 %hidden_gradient.3 = bf16[64,256]{1,0:T(8,128)(2,1)} custom-call(bf16[64,6144]{1,0:T(8,128)(2,1)} %weights_hbm.3, bf16[256,6144]{1,0:T(8,128)(2,1)S(1)} %get-tuple-element.27.grads, bf16[64,256]{1,0:T(8,128)(2,1)} %hidden_gradient.2.refs_0_), custom_call_target="tpu_custom_call", output_to_operand_aliasing={{}: (2, {})} | custom-call | flops 201326592 | bytes 3932160 | tf_op jit(solution)/shard_map/hidden_gradient/pallas_call | solution.py:228
  35.6 0.9 %new_states.1 = (f32[8,6144]{1,0:T(8,128)}, f32[8,6144]{1,0:T(8,128)}, f32[8,6144]{1,0:T(8,128)}) custom-call(f32[2,128]{1,0:T(2,128)S(1)} %broadcast_in_dim.4.fix_ref, f32[8,6144]{1,0:T(8,128)S(1)} %get-tuple-element.28.refs_4_.master, f32[8,6144]{1,0:T(8,128)S(1)} %get-tuple-element.29.refs_5_.first, f32[8,6144]{1,0:T(8,128)S(1)} %get-tuple-element.30.refs_6_.second, ...), custom_call_target="tpu_custom_call" | custom-call | flops 983040 | bytes 1376256 | tf_op jit(solution)/shard_map/new_states/pallas_call | solution.py:309
  36.5 0.0 collective-permute-done.12.refs_9_
  36.5 0.0 collective-permute-done.7.refs_4_
  36.5 0.0 collective-permute-done.10.refs_7_
  36.5 0.0 collective-permute-done.9.refs_6_
  36.5 0.0 collective-permute-done.8.refs_5_
  36.5 0.0 copy-done
  36.5 1.7 %place.1 = (bf16[64,6144]{1,0:T(8,128)(2,1)}, f32[3,8,6144]{2,1,0:T(8,128)}) custom-call(s32[8]{0:T(128)S(1)} %copy-done, bf16[8,6144]{1,0:T(8,128)(2,1)S(1)} %get-tuple-element.41.refs_0_, bf16[8,6144]{1,0:T(8,128)(2,1)S(1)} %collective-permute-done.4.refs_1_, bf16[8,6144]{1,0:T(8,128)(2,1)S(1)} %collective-permute-done.5.refs_2_, ...), custom_call_target="tpu_custom_call" | custom-call | bytes 3145728 | tf_op jit(solution)/shard_map/place/pallas_call | solution.py:360
  (1 shorter events, 0.0 us)
Async XLA Ops:
  2.9 2.3 %collective-permute-start = (bf16[32,6144]{1,0:T(8,128)(2,1)S(1)}, bf16[32,6144]{1,0:T(8,128)(2,1)S(1)}, u32[]{:S(2)}, u32[]{:S(2)}) collective-permute-start(bf16[32,6144]{1,0:T(8,128)(2,1)S(1)} %get-tuple-element.32), channel_id=1, source_target_pairs={{0,1},{1,0},{2,3},{3,2},{4,5},{5,4},{6,7},{7,6},{8,9},{9,8},{10,11... | collective-permute-start | bytes 1179656 | tf_op jit(solution)/shard_map/ppermute | solution.py:386
  3.4 20.6 %collective-permute-start.11 = (bf16[16,6144]{1,0:T(8,128)(2,1)S(1)}, bf16[16,6144]{1,0:T(8,128)(2,1)S(1)}, u32[]{:S(2)}, u32[]{:S(2)}) collective-permute-start(bf16[16,6144]{1,0:T(8,128)(2,1)S(1)} %get-tuple-element.42), channel_id=1, source_target_pairs={{0,1},{1,2},{2,3},{3,4},{4,5},{5,6},{6,7},{7,0},{8,9},{9,10},{10,1... | collective-permute-start | bytes 589832 | tf_op jit(solution)/shard_map/ppermute | solution.py:386
  5.3 8.4 %collective-permute-start.1 = (bf16[8,6144]{1,0:T(8,128)(2,1)S(1)}, bf16[8,6144]{1,0:T(8,128)(2,1)S(1)}, u32[]{:S(2)}, u32[]{:S(2)}) collective-permute-start(bf16[8,6144]{1,0:T(8,128)(2,1)S(1)} %get-tuple-element.34), channel_id=1, source_target_pairs={{0,4},{1,3},{2,6},{3,1},{4,0},{5,7},{6,2},{7,5},{8,12},{9,11},{10,... | collective-permute-start | bytes 294920 | tf_op jit(solution)/shard_map/ppermute | solution.py:386
  9.4 7.5 %collective-permute-start.2 = (bf16[8,6144]{1,0:T(8,128)(2,1)S(1)}, bf16[8,6144]{1,0:T(8,128)(2,1)S(1)}, u32[]{:S(2)}, u32[]{:S(2)}) collective-permute-start(bf16[8,6144]{1,0:T(8,128)(2,1)S(1)} %get-tuple-element.35), channel_id=1, source_target_pairs={{0,6},{1,5},{2,4},{3,7},{4,2},{5,1},{6,0},{7,3},{8,14},{9,13},{10,... | collective-permute-start | bytes 294920 | tf_op jit(solution)/shard_map/ppermute | solution.py:386
  10.7 6.1 %collective-permute-start.3 = (bf16[8,6144]{1,0:T(8,128)(2,1)S(1)}, bf16[8,6144]{1,0:T(8,128)(2,1)S(1)}, u32[]{:S(2)}, u32[]{:S(2)}) collective-permute-start(bf16[8,6144]{1,0:T(8,128)(2,1)S(1)} %get-tuple-element.36), channel_id=1, source_target_pairs={{0,2},{1,7},{2,0},{3,5},{4,6},{5,3},{6,4},{7,1},{8,10},{9,15},{10,... | collective-permute-start | bytes 294920 | tf_op jit(solution)/shard_map/ppermute | solution.py:386
  17.2 7.3 %collective-permute-start.6 = (bf16[8,6144]{1,0:T(8,128)(2,1)S(1)}, bf16[8,6144]{1,0:T(8,128)(2,1)S(1)}, u32[]{:S(2)}, u32[]{:S(2)}) collective-permute-start(bf16[8,6144]{1,0:T(8,128)(2,1)S(1)} %get-tuple-element.41.refs_0_), channel_id=1, source_target_pairs={{0,2},{1,7},{2,0},{3,5},{4,6},{5,3},{6,4},{7,1},{8,10},{9,15},{10,... | collective-permute-start | bytes 294920 | tf_op jit(solution)/shard_map/ppermute | solution.py:386
  20.6 8.8 %collective-permute-start.5 = (bf16[8,6144]{1,0:T(8,128)(2,1)S(1)}, bf16[8,6144]{1,0:T(8,128)(2,1)S(1)}, u32[]{:S(2)}, u32[]{:S(2)}) collective-permute-start(bf16[8,6144]{1,0:T(8,128)(2,1)S(1)} %get-tuple-element.41.refs_0_), channel_id=1, source_target_pairs={{0,6},{1,5},{2,4},{3,7},{4,2},{5,1},{6,0},{7,3},{8,14},{9,13},{10,... | collective-permute-start | bytes 294920 | tf_op jit(solution)/shard_map/ppermute | solution.py:386
  24.0 8.6 %collective-permute-start.4 = (bf16[8,6144]{1,0:T(8,128)(2,1)S(1)}, bf16[8,6144]{1,0:T(8,128)(2,1)S(1)}, u32[]{:S(2)}, u32[]{:S(2)}) collective-permute-start(bf16[8,6144]{1,0:T(8,128)(2,1)S(1)} %get-tuple-element.41.refs_0_), channel_id=1, source_target_pairs={{0,4},{1,3},{2,6},{3,1},{4,0},{5,7},{6,2},{7,5},{8,12},{9,11},{10,... | collective-permute-start | bytes 294920 | tf_op jit(solution)/shard_map/ppermute | solution.py:386
  24.0 12.5 %collective-permute-start.7 = (bf16[8,6144]{1,0:T(8,128)(2,1)S(1)}, bf16[8,6144]{1,0:T(8,128)(2,1)S(1)}, u32[]{:S(2)}, u32[]{:S(2)}) collective-permute-start(bf16[8,6144]{1,0:T(8,128)(2,1)S(1)} %get-tuple-element.41.refs_0_), channel_id=1, source_target_pairs={{0,1},{1,0},{2,3},{3,2},{4,5},{5,4},{6,7},{7,6},{8,9},{9,8},{10,11... | collective-permute-start | bytes 294920 | tf_op jit(solution)/shard_map/ppermute | solution.py:386
  24.0 12.5 %collective-permute-start.12 = (bf16[8,6144]{1,0:T(8,128)(2,1)S(1)}, bf16[8,6144]{1,0:T(8,128)(2,1)S(1)}, u32[]{:S(2)}, u32[]{:S(2)}) collective-permute-start(bf16[8,6144]{1,0:T(8,128)(2,1)S(1)} %get-tuple-element.43), channel_id=1, source_target_pairs={{0,1},{1,2},{2,3},{3,4},{4,5},{5,6},{6,7},{7,0},{8,9},{9,10},{10,1... | collective-permute-start | bytes 294920 | tf_op jit(solution)/shard_map/ppermute | solution.py:386
  24.5 11.9 %collective-permute-start.10 = (bf16[8,6144]{1,0:T(8,128)(2,1)S(1)}, bf16[8,6144]{1,0:T(8,128)(2,1)S(1)}, u32[]{:S(2)}, u32[]{:S(2)}) collective-permute-start(bf16[8,6144]{1,0:T(8,128)(2,1)S(1)} %collective-permute-done.6.refs_3_), channel_id=1, source_target_pairs={{0,1},{1,0},{2,3},{3,2},{4,5},{5,4},{6,7},{7,6},{8,9},{9,8},{10,11... | collective-permute-start | bytes 294920 | tf_op jit(solution)/shard_map/ppermute | solution.py:386
  29.4 7.1 %collective-permute-start.9 = (bf16[8,6144]{1,0:T(8,128)(2,1)S(1)}, bf16[8,6144]{1,0:T(8,128)(2,1)S(1)}, u32[]{:S(2)}, u32[]{:S(2)}) collective-permute-start(bf16[8,6144]{1,0:T(8,128)(2,1)S(1)} %collective-permute-done.5.refs_2_), channel_id=1, source_target_pairs={{0,1},{1,0},{2,3},{3,2},{4,5},{5,4},{6,7},{7,6},{8,9},{9,8},{10,11... | collective-permute-start | bytes 294920 | tf_op jit(solution)/shard_map/ppermute | solution.py:386
  32.7 3.8 %collective-permute-start.8 = (bf16[8,6144]{1,0:T(8,128)(2,1)S(1)}, bf16[8,6144]{1,0:T(8,128)(2,1)S(1)}, u32[]{:S(2)}, u32[]{:S(2)}) collective-permute-start(bf16[8,6144]{1,0:T(8,128)(2,1)S(1)} %collective-permute-done.4.refs_1_), channel_id=1, source_target_pairs={{0,1},{1,0},{2,3},{3,2},{4,5},{5,4},{6,7},{7,6},{8,9},{9,8},{10,11... | collective-permute-start | bytes 294920 | tf_op jit(solution)/shard_map/ppermute | solution.py:386
  32.7 3.8 %copy-start = (s32[8]{0:T(128)S(1)}, s32[8]{0:T(128)}, u32[]{:S(2)}) copy-start(s32[8]{0:T(128)} %order.1) | copy-start | bytes 100

commit v2 on v1

--- a/solution.py
+++ b/solution.py
@@ -1,4 +1,5 @@
 import functools
+import math
 
 import jax
 import jax.numpy as jnp
@@ -77,19 +78,35 @@
     return lax.axis_index("replica") % 2
 
 
-def distances_of(chips, core):
-    ks = sorted(range(1, chips), key=lambda k: (k ^ (chips >> 1), k))
-    return [0] + (ks[-1:] + ks[:-1] if core else ks)
-
-
-def distance_at(place, chips, core):
-    first, second = (distances_of(chips, c)[place] for c in range(2))
+SUM_MOVES = ((("xor", 2), ("xor", 1), ("xor", 3)), (("xor", 1), ("xor", 2), ("xor", 3)))
+GATHER_MOVES = ((("xor", 2), ("xor", 1), ("xor", 3)), (("xor", 2), ("xor", 1), ("xor", 3)))
+
+
+def move_of(moves, chips, core, place):
+    if place == 0:
+        return ("on", 0)
+    return moves[core][place - 1] if len(moves[core]) == chips - 1 else ("on", place)
+
+
+def moved_chip(chip, chips, move, back=False):
+    kind, by = move
+    if kind == "xor":
+        return chip ^ by
+    by = chips - by if back else by
+    return lax.rem(chip + by, chips) if isinstance(chip, jax.Array) else (chip + by) % chips
+
+
+def owner_at(place, chips, core, moves, back):
+    chip = lax.axis_index("replica") // 2
+    first, second = (
+        2 * moved_chip(chip, chips, move_of(moves, chips, c, place), back) + c for c in range(2)
+    )
     return jnp.where(core == 0, first, second)
 
 
 def send_kernel(
     order_hbm, acts_hbm, grads_hbm, first_hbm, second_hbm,
-    send_ref, grads, picked, first, second, moments, order, acts, sems,
+    send_ref, grads, picked, first, second, moments, table, order, acts, sems,
 ):
     replicas = order.shape[0]
     rows, tokens = acts.shape
@@ -111,8 +128,7 @@
     ]
     for copy in small + tiles + states:
         copy.start()
-    me = lax.axis_index("replica")
-    chip, core = me // 2, me % 2
+    core = this_core()
     at = lax.broadcasted_iota(jnp.int32, (rows, rows), 0)
     column = lax.broadcasted_iota(jnp.int32, (rows, rows), 1)
     source = at
@@ -121,12 +137,19 @@
     for place in range(replicas):
         at_place, mine = place % (replicas // 2), place // (replicas // 2)
         lane = core if mine else 1 - core
-        owner = 2 * (chip ^ distance_at(at_place, replicas // 2, lane)) + lane
+        owner = owner_at(at_place, replicas // 2, lane, SUM_MOVES, False)
         inside = (at >= place * block) & (at < (place + 1) * block)
         source = jnp.where(inside, at + (order[owner] - place) * block, source)
     chosen = jnp.where(column == source, 1.0, 0.0).astype(acts.dtype)
     both = jnp.dot(chosen, acts[...], preferred_element_type=jnp.float32).astype(picked.dtype)
     picked[...] = both[half:]
+    line = lax.broadcasted_iota(jnp.int32, table.shape, 0)
+    value = jnp.zeros(table.shape, jnp.int32)
+    for place in range(replicas):
+        at_place, far = place % (replicas // 2), place // (replicas // 2)
+        owner = owner_at(at_place, replicas // 2, 1 - core if far else core, GATHER_MOVES, True)
+        value = jnp.where(line == place, order[owner] * block, value)
+    table[...] = value
     mine = both[:half]
     for copy, span in zip(tiles, spans):
         copy.wait()
@@ -144,7 +167,7 @@
     return pl.pallas_call(
         send_kernel,
         in_specs=[HBM()] * 5,
-        out_specs=[VMEM()] * 6,
+        out_specs=[VMEM()] * 7,
         out_shape=[
             jax.ShapeDtypeStruct((rows // 2, width), jnp.bfloat16),
             jax.ShapeDtypeStruct((tokens, width), grads_out.dtype),
@@ -152,6 +175,7 @@
             jax.ShapeDtypeStruct((block, width), jnp.float32),
             jax.ShapeDtypeStruct((block, width), jnp.float32),
             jax.ShapeDtypeStruct((2 * block, width), jnp.bfloat16),
+            jax.ShapeDtypeStruct((order.shape[0], 128), jnp.int32),
         ],
         scratch_shapes=[
             pltpu.SMEM(order.shape, order.dtype),
@@ -266,7 +290,25 @@
     )(keep, got)
 
 
-def update_kernel(fix_ref, *refs):
+def rates_kernel(count, out):
+    line = lax.broadcasted_iota(jnp.int32, out.shape, 0)
+    log = jnp.where(line < out.shape[0] // 2, math.log(0.9), math.log(0.95))
+    out[...] = 1.0 - jnp.exp(count[0].astype(jnp.float32) * log)
+
+
+def corrections(count):
+    return pl.pallas_call(
+        rates_kernel,
+        in_specs=[SMEM()],
+        out_specs=VMEM(),
+        out_shape=jax.ShapeDtypeStruct((16, 128), jnp.float32),
+        compiler_params=params(),
+        cost_estimate=cost(0, 8192),
+        name="corrections",
+    )(count)
+
+
+def update_kernel(fix, *refs):
     parts, (master, first, second, grads_ref, send_master, send_grads) = refs[:-6], refs[-6:]
     grads = parts[0][...]
     for part in parts[1:]:
@@ -274,7 +316,7 @@
     grads_ref[...] = grads
     send_grads[...] = grads.astype(send_grads.dtype)
     new_master, _, _ = adam_update(
-        grads, master[...], first[...], second[...], fix_ref[0:1, 0:1], fix_ref[1:2, 0:1]
+        grads, master[...], first[...], second[...], fix[0:1, 0:1], fix[8:9, 0:1]
     )
     send_master[...] = new_master.astype(send_master.dtype)
 
@@ -296,9 +338,9 @@
     )(fix, *parts, *states)
 
 
-def states_kernel(fix_ref, master, first, second, grads, *outs):
+def states_kernel(fix, master, first, second, grads, *outs):
     updated = adam_update(
-        grads[...], master[...], first[...], second[...], fix_ref[0:1, 0:1], fix_ref[1:2, 0:1]
+        grads[...], master[...], first[...], second[...], fix[0:1, 0:1], fix[8:9, 0:1]
     )
     for out, value in zip(outs, updated):
         out[...] = value
@@ -317,24 +359,18 @@
     )(fix, *states, grads)
 
 
-def owner_at(place, chips, sibling):
-    me = lax.axis_index("replica")
-    lane = 1 - me % 2 if sibling else me % 2
-    return 2 * (me // 2 ^ distance_at(place, chips, lane)) + lane
-
-
-def place_kernel(chips, order, *refs):
+def place_kernel(chips, table, *refs):
     near, far = refs[:chips], refs[chips : 2 * chips]
     packed, moved, weights, checkpoint, partner, sems = refs[2 * chips :]
     block = moved.shape[0]
-    replicas = order.shape[0]
-    previous = lax.rem(lax.axis_index("replica") + replicas - 1, replicas)
+    replicas = 2 * chips
+    me = lax.axis_index("replica")
+    previous = lax.rem(me + replicas - 1, replicas)
+    rows = table[...]
     copies = []
-    for sibling, pieces in enumerate((near, far)):
-        for at, piece in enumerate(pieces):
-            row = pl.multiple_of(order[owner_at(at, chips, sibling)] * block, block)
-            target = weights.at[pl.ds(row, block), :]
-            copies.append(pltpu.make_async_copy(piece, target, sems.at[len(copies)]))
+    for at, piece in enumerate((*near, *far)):
+        target = weights.at[pl.ds(pl.multiple_of(rows[at, 0], block), block), :]
+        copies.append(pltpu.make_async_copy(piece, target, sems.at[at]))
     for copy in copies:
         copy.start()
     grads = moved[...].astype(jnp.float32)
@@ -342,7 +378,7 @@
     partner[2] = 0.95 * packed[block:].astype(jnp.float32) + 0.05 * grads * grads
     for at, piece in enumerate(far):
 
-        @pl.when(owner_at(at, chips, 1) == previous)
+        @pl.when(owner_at(at, chips, 1 - me % 2, GATHER_MOVES, True) == previous)
         def _():
             partner[0] = piece[...].astype(jnp.float32)
 
@@ -353,13 +389,13 @@
     last.wait()
 
 
-def place(order, near, far, packed, moved):
+def place(table, near, far, packed, moved):
     block, width = moved.shape
     chips = len(near)
     rows = 2 * chips * block
     return pl.pallas_call(
         functools.partial(place_kernel, chips),
-        in_specs=[SMEM()] + [VMEM()] * (2 * chips + 2),
+        in_specs=[VMEM()] * (2 * chips + 3),
         out_specs=[HBM()] * 2,
         out_shape=[
             jax.ShapeDtypeStruct((rows, width), jnp.bfloat16),
@@ -372,7 +408,7 @@
         compiler_params=params(),
         cost_estimate=cost(0, 8 * rows * width),
         name="place",
-    )(order, *near, *far, packed, moved)
+    )(table, *near, *far, packed, moved)
 
 
 def tiled_device(
@@ -385,9 +421,11 @@
     def permuted(piece, target):
         return lax.ppermute(piece, "replica", [(i, target(i)) for i in range(replicas)])
 
-    def across(piece, at):
-        ks = [distances_of(chips, core)[at] for core in range(2)]
-        return permuted(piece, lambda i: i ^ (2 * ks[i % 2]))
+    def across(piece, at, moves):
+        def target(i):
+            return 2 * moved_chip(i // 2, chips, move_of(moves, chips, i % 2, at)) + i % 2
+
+        return permuted(piece, target)
 
     def to_sibling(piece):
         return permuted(piece, lambda i: i ^ 1)
@@ -395,11 +433,7 @@
     def along_ring(piece):
         return permuted(piece, lambda i: (i + 1) % replicas)
 
-    steps = step_count[0].astype(jnp.float32)
-    fix = jnp.stack([1.0 - jnp.power(0.9, steps), 1.0 - jnp.power(0.95, steps)])
-    fix = jnp.broadcast_to(fix[:, None], (2, 128))
-
-    send, grads_out, picked, first, second, packed = slab_to_send(
+    send, grads_out, picked, first, second, packed, table = slab_to_send(
         owner_order, hidden[0].T, out_grad[0], first_moment, second_moment, 4
     )
     got = to_sibling(send)
@@ -409,13 +443,14 @@
     own, *sends = pair_sum(keep, got, block)
     hidden_grad = hidden_gradient(weights_old, grads_out, 1, 2)
     hidden_grad = hidden_gradient(weights_old, grads_out, 0, 2, (hidden_grad,))
-    parts = [own] + [across(sends[k - 1], k) for k in range(1, chips)]
+    parts = [own] + [across(sends[k - 1], k, SUM_MOVES) for k in range(1, chips)]
+    fix = corrections(lax.optimization_barrier((step_count, own))[0])
     grads, send_master, send_grads = update(fix, parts, states)
-    near = [send_master] + [across(send_master, k) for k in range(1, chips)]
+    near = [send_master] + [across(send_master, k, GATHER_MOVES) for k in range(1, chips)]
     updated = new_states(fix, states, grads)
     moved = along_ring(send_grads)
     far = [to_sibling(piece) for piece in near]
-    weights_new, checkpoint = place(owner_order, near, far, packed, moved)
+    weights_new, checkpoint = place(table, near, far, packed, moved)
     return (*updated, checkpoint, weights_new, hidden_grad.T[None])
 
 

time: 38.4 us -> 37.7 us (0.982)
  starting transfers between devices: 17.1 us -> 11.4 us
  waiting for transfers between devices: 10.5 us -> 15.9 us
  Pallas kernels: 9.03 us -> 8.51 us
    ppermute x13, starting transfers between devices: 17.1 us -> 11.4 us  [permuted(): lax.ppermute(piece, 'replica', [(i, target(i)) for i in range(replicas)])]
    ppermute x13, waiting for transfers between devices: 10.5 us -> 15.9 us  [permuted(): lax.ppermute(piece, 'replica', [(i, target(i)) for i in range(replicas)])]
    pallas_call x2 -> x3, Pallas kernels: 3.97 us -> 3.46 us  [the longest x1 2.25 us: slab_to_send(): pl.pallas_call(send_kernel, in_specs=[HBM()] * 5, out_specs=[VMEM()] * 7,...]
  transfers between devices with their start and end apart: 13 -> 13, of which waited for: 4 -> 7; matrix products, arithmetic and copies ran while one was open for 0% -> 0% of each run, Pallas kernels for 13% -> 13%
where the time goes in v2:
time: 37.7 us; the launch traced here: 37.2 us
  waiting for transfers between devices  15.9 us (42%)
  starting transfers between devices  11.4 us (30%)
  Pallas kernels  8.51 us (23%)
  between operations  1.37 us (4%)
    ppermute x13, waiting for transfers between devices, permuted(): lax.ppermute(piece, 'replica', [(i, target(i)) for i in range(replicas)])  15.9 us
    ppermute x13, starting transfers between devices, permuted(): lax.ppermute(piece, 'replica', [(i, target(i)) for i in range(replicas)])  11.4 us
    pallas_call x2, Pallas kernels, hidden_gradient(): pl.pallas_call(functools.partial(back_kernel, width ** (-0.5), core), in_...  2.88 us
    pallas_call x1, Pallas kernels, slab_to_send(): pl.pallas_call(send_kernel, in_specs=[HBM()] * 5, out_specs=[VMEM()] * 7,...  2.25 us
    pallas_call x1, Pallas kernels, place(): pl.pallas_call(functools.partial(place_kernel, chips), in_specs=[VMEM()]...  1.2 us
    pallas_call x1, Pallas kernels, slab_to_keep(): pl.pallas_call(keep_kernel, in_specs=[VMEM()] * 2 + [HBM()], out_specs=[V...  0.93 us
    pallas_call x1, Pallas kernels, new_states(): pl.pallas_call(states_kernel, in_specs=[VMEM()] * 5, out_specs=[VMEM()] *...  0.9 us
  transfers between devices with their start and end apart: 13, of which 7 were waited for; matrix products, arithmetic and copies ran while one was open for 0% of the time, Pallas kernels for 13%

profile of v2, /device:TPU:0, one launch (start us, length us, event | category | flops | bytes accessed | tf_op | source)
XLA Modules:
  0.0 37.2 jit_solution(2102161956151484605)
XLA Ops:
  0.6 2.2 %slab_to_send.1 = (bf16[32,6144]{1,0:T(8,128)(2,1)S(1)}, bf16[256,6144]{1,0:T(8,128)(2,1)S(1)}, bf16[32,256]{1,0:T(8,128)(2,1)S(1)}, f32[8,6144]{1,0:T(8,128)S(1...) custom-call(s32[8]{0:T(128)} %order_hbm.1, bf16[64,256]{1,0:T(8,128)(2,1)} %bitcast.9, ...), custom_call_target="tpu_custom_call" | custom-call | flops 100663296 | bytes 3145728 | tf_op jit(solution)/shard_map/slab_to_send/pallas_call | solution.py:167
  2.9 0.6 %collective-permute-start = (bf16[32,6144]{1,0:T(8,128)(2,1)S(1)}, bf16[32,6144]{1,0:T(8,128)(2,1)S(1)}, u32[]{:S(2)}, u32[]{:S(2)}) collective-permute-start(bf16[32,6144]{1,0:T(8,128)(2,1)S(1)} %get-tuple-element.31), channel_id=1, source_target_pairs={{0,1},{1,0},{2,3},{3,2},{4,5},{5,4},{6,7},{7,6},{8,9},{9,8},{10,11... | collective-permute-start | bytes 1179656 | tf_op jit(solution)/shard_map/ppermute | solution.py:422
  3.4 0.9 %slab_to_keep.1 = (f32[32,6144]{1,0:T(8,128)S(1)}, f32[8,6144]{1,0:T(8,128)S(1)}) custom-call(bf16[32,256]{1,0:T(8,128)(2,1)S(1)} %get-tuple-element.28.picked, bf16[256,6144]{1,0:T(8,128)(2,1)S(1)} %get-tuple-element.29.grads, f32[8,6144]{1,0:T(8,128)} %master_hbm.1), custom_call_target="tpu_custom_call" | custom-call | flops 100663296 | bytes 3145728 | tf_op jit(solution)/shard_map/slab_to_keep/pallas_call | solution.py:206
  4.4 0.4 %collective-permute-done.got_ref = bf16[32,6144]{1,0:T(8,128)(2,1)S(1)} collective-permute-done((bf16[32,6144]{1,0:T(8,128)(2,1)S(1)}, bf16[32,6144]{1,0:T(8,128)(2,1)S(1)}, u32[]{:S(2)}, u32[]{:S(2)}) %collective-permute-start) | collective-permute-done | bytes 393248 | tf_op jit(solution)/shard_map/ppermute | solution.py:422
  4.8 0.1 pair_sum.1
  4.9 4.0 %collective-permute-start.1 = (bf16[8,6144]{1,0:T(8,128)(2,1)S(1)}, bf16[8,6144]{1,0:T(8,128)(2,1)S(1)}, u32[]{:S(2)}, u32[]{:S(2)}) collective-permute-start(bf16[8,6144]{1,0:T(8,128)(2,1)S(1)} %get-tuple-element.37), channel_id=1, source_target_pairs={{0,4},{1,3},{2,6},{3,1},{4,0},{5,7},{6,2},{7,5},{8,12},{9,11},{10,... | collective-permute-start | bytes 294920 | tf_op jit(solution)/shard_map/ppermute | solution.py:422
  8.9 1.6 %collective-permute-start.2 = (bf16[8,6144]{1,0:T(8,128)(2,1)S(1)}, bf16[8,6144]{1,0:T(8,128)(2,1)S(1)}, u32[]{:S(2)}, u32[]{:S(2)}) collective-permute-start(bf16[8,6144]{1,0:T(8,128)(2,1)S(1)} %get-tuple-element.38), channel_id=1, source_target_pairs={{0,2},{1,5},{2,0},{3,7},{4,6},{5,1},{6,4},{7,3},{8,10},{9,13},{10,... | collective-permute-start | bytes 294920 | tf_op jit(solution)/shard_map/ppermute | solution.py:422
  10.5 0.0 collective-permute-start.3
  10.5 0.0 collective-permute-start.11
  11.1 0.6 %collective-permute-done.1.refs_1_ = bf16[8,6144]{1,0:T(8,128)(2,1)S(1)} collective-permute-done((bf16[8,6144]{1,0:T(8,128)(2,1)S(1)}, bf16[8,6144]{1,0:T(8,128)(2,1)S(1)}, u32[]{:S(2)}, u32[]{:S(2)}) %collective-permute-start.1) | collective-permute-done | bytes 98336 | tf_op jit(solution)/shard_map/ppermute | solution.py:422
  11.7 2.0 %collective-permute-done.2.refs_2_ = bf16[8,6144]{1,0:T(8,128)(2,1)S(1)} collective-permute-done((bf16[8,6144]{1,0:T(8,128)(2,1)S(1)}, bf16[8,6144]{1,0:T(8,128)(2,1)S(1)}, u32[]{:S(2)}, u32[]{:S(2)}) %collective-permute-start.2) | collective-permute-done | bytes 98336 | tf_op jit(solution)/shard_map/ppermute | solution.py:422
  13.8 4.4 %collective-permute-done.3.refs_3_ = bf16[8,6144]{1,0:T(8,128)(2,1)S(1)} collective-permute-done((bf16[8,6144]{1,0:T(8,128)(2,1)S(1)}, bf16[8,6144]{1,0:T(8,128)(2,1)S(1)}, u32[]{:S(2)}, u32[]{:S(2)}) %collective-permute-start.3) | collective-permute-done | bytes 98336 | tf_op jit(solution)/shard_map/ppermute | solution.py:422
  18.1 0.3 update.1
  18.4 2.6 %collective-permute-start.6 = (bf16[8,6144]{1,0:T(8,128)(2,1)S(1)}, bf16[8,6144]{1,0:T(8,128)(2,1)S(1)}, u32[]{:S(2)}, u32[]{:S(2)}) collective-permute-start(bf16[8,6144]{1,0:T(8,128)(2,1)S(1)} %get-tuple-element.45.refs_0_), channel_id=1, source_target_pairs={{0,6},{1,7},{2,4},{3,5},{4,2},{5,3},{6,0},{7,1},{8,14},{9,15},{10,... | collective-permute-start | bytes 294920 | tf_op jit(solution)/shard_map/ppermute | solution.py:422
  21.0 1.8 %collective-permute-start.5 = (bf16[8,6144]{1,0:T(8,128)(2,1)S(1)}, bf16[8,6144]{1,0:T(8,128)(2,1)S(1)}, u32[]{:S(2)}, u32[]{:S(2)}) collective-permute-start(bf16[8,6144]{1,0:T(8,128)(2,1)S(1)} %get-tuple-element.45.refs_0_), channel_id=1, source_target_pairs={{0,2},{1,3},{2,0},{3,1},{4,6},{5,7},{6,4},{7,5},{8,10},{9,11},{10,... | collective-permute-start | bytes 294920 | tf_op jit(solution)/shard_map/ppermute | solution.py:422
  22.8 0.2 collective-permute-start.4
  23.0 0.0 collective-permute-start.7
  23.0 0.0 collective-permute-done.11.refs_8_
  23.0 0.5 %collective-permute-start.12 = (bf16[8,6144]{1,0:T(8,128)(2,1)S(1)}, bf16[8,6144]{1,0:T(8,128)(2,1)S(1)}, u32[]{:S(2)}, u32[]{:S(2)}) collective-permute-start(bf16[8,6144]{1,0:T(8,128)(2,1)S(1)} %get-tuple-element.47), channel_id=1, source_target_pairs={{0,1},{1,2},{2,3},{3,4},{4,5},{5,6},{6,7},{7,0},{8,9},{9,10},{10,1... | collective-permute-start | bytes 294920 | tf_op jit(solution)/shard_map/ppermute | solution.py:422
  23.5 1.5 %collective-permute-done.6.refs_3_ = bf16[8,6144]{1,0:T(8,128)(2,1)S(1)} collective-permute-done((bf16[8,6144]{1,0:T(8,128)(2,1)S(1)}, bf16[8,6144]{1,0:T(8,128)(2,1)S(1)}, u32[]{:S(2)}, u32[]{:S(2)}) %collective-permute-start.6) | collective-permute-done | bytes 98336 | tf_op jit(solution)/shard_map/ppermute | solution.py:422
  25.0 0.1 collective-permute-start.10
  25.1 1.2 %collective-permute-done.5.refs_2_ = bf16[8,6144]{1,0:T(8,128)(2,1)S(1)} collective-permute-done((bf16[8,6144]{1,0:T(8,128)(2,1)S(1)}, bf16[8,6144]{1,0:T(8,128)(2,1)S(1)}, u32[]{:S(2)}, u32[]{:S(2)}) %collective-permute-start.5) | collective-permute-done | bytes 98336 | tf_op jit(solution)/shard_map/ppermute | solution.py:422
  26.3 0.0 collective-permute-start.9
  26.3 5.8 %collective-permute-done.4.refs_1_ = bf16[8,6144]{1,0:T(8,128)(2,1)S(1)} collective-permute-done((bf16[8,6144]{1,0:T(8,128)(2,1)S(1)}, bf16[8,6144]{1,0:T(8,128)(2,1)S(1)}, u32[]{:S(2)}, u32[]{:S(2)}) %collective-permute-start.4) | collective-permute-done | bytes 98336 | tf_op jit(solution)/shard_map/ppermute | solution.py:422
  32.1 0.0 collective-permute-start.8
  32.2 2.9 %hidden_gradient.3 = bf16[64,256]{1,0:T(8,128)(2,1)} custom-call(bf16[64,6144]{1,0:T(8,128)(2,1)} %weights_hbm.3, bf16[256,6144]{1,0:T(8,128)(2,1)S(1)} %get-tuple-element.29.grads, bf16[64,256]{1,0:T(8,128)(2,1)} %hidden_gradient.2.refs_0_), custom_call_target="tpu_custom_call", output_to_operand_aliasing={{}: (2, {})} | custom-call | flops 201326592 | bytes 3932160 | tf_op jit(solution)/shard_map/hidden_gradient/pallas_call | solution.py:252
  35.0 0.9 %new_states.1 = (f32[8,6144]{1,0:T(8,128)}, f32[8,6144]{1,0:T(8,128)}, f32[8,6144]{1,0:T(8,128)}) custom-call(f32[16,128]{1,0:T(8,128)S(1)} %corrections.1.fix, f32[8,6144]{1,0:T(8,128)S(1)} %get-tuple-element.34.refs_4_.master, f32[8,6144]{1,0:T(8,128)S(1)} %get-tuple-element.35.refs_5_.first, f32[8,6144]{1,0:T(8,128)S(1)} %get-tuple-element.36.refs_6_.second, ...), custom_call_target="tpu_custom_call" | custom-call | flops 983040 | bytes 1376256 | tf_op jit(solution)/shard_map/new_states/pallas_call | solution.py:351
  35.9 0.0 collective-permute-done.12.refs_9_
  35.9 0.0 collective-permute-done.7.refs_4_
  35.9 0.0 collective-permute-done.10.refs_7_
  36.0 0.0 collective-permute-done.9.refs_6_
  36.0 0.0 collective-permute-done.8.refs_5_
  36.0 1.2 %place.1 = (bf16[64,6144]{1,0:T(8,128)(2,1)}, f32[3,8,6144]{2,1,0:T(8,128)}) custom-call(s32[8,128]{1,0:T(8,128)S(1)} %get-tuple-element.44.table, bf16[8,6144]{1,0:T(8,128)(2,1)S(1)} %get-tuple-element.45.refs_0_, bf16[8,6144]{1,0:T(8,128)(2,1)S(1)} %collective-permute-done.4.refs_1_, bf16[8,6144]{1,0:T(8,128)(2,1)S(1)} %collective-permute-done.5.refs_2_, ...), custom_call_target="tpu_custom_call" | custom-call | bytes 3145728 | tf_op jit(solution)/shard_map/place/pallas_call | solution.py:396
  (2 shorter events, 0.0 us)
Async XLA Ops:
  2.9 1.9 %collective-permute-start = (bf16[32,6144]{1,0:T(8,128)(2,1)S(1)}, bf16[32,6144]{1,0:T(8,128)(2,1)S(1)}, u32[]{:S(2)}, u32[]{:S(2)}) collective-permute-start(bf16[32,6144]{1,0:T(8,128)(2,1)S(1)} %get-tuple-element.31), channel_id=1, source_target_pairs={{0,1},{1,0},{2,3},{3,2},{4,5},{5,4},{6,7},{7,6},{8,9},{9,8},{10,11... | collective-permute-start | bytes 1179656 | tf_op jit(solution)/shard_map/ppermute | solution.py:422
  4.9 6.9 %collective-permute-start.1 = (bf16[8,6144]{1,0:T(8,128)(2,1)S(1)}, bf16[8,6144]{1,0:T(8,128)(2,1)S(1)}, u32[]{:S(2)}, u32[]{:S(2)}) collective-permute-start(bf16[8,6144]{1,0:T(8,128)(2,1)S(1)} %get-tuple-element.37), channel_id=1, source_target_pairs={{0,4},{1,3},{2,6},{3,1},{4,0},{5,7},{6,2},{7,5},{8,12},{9,11},{10,... | collective-permute-start | bytes 294920 | tf_op jit(solution)/shard_map/ppermute | solution.py:422
  8.9 4.9 %collective-permute-start.2 = (bf16[8,6144]{1,0:T(8,128)(2,1)S(1)}, bf16[8,6144]{1,0:T(8,128)(2,1)S(1)}, u32[]{:S(2)}, u32[]{:S(2)}) collective-permute-start(bf16[8,6144]{1,0:T(8,128)(2,1)S(1)} %get-tuple-element.38), channel_id=1, source_target_pairs={{0,2},{1,5},{2,0},{3,7},{4,6},{5,1},{6,4},{7,3},{8,10},{9,13},{10,... | collective-permute-start | bytes 294920 | tf_op jit(solution)/shard_map/ppermute | solution.py:422
  10.5 7.7 %collective-permute-start.3 = (bf16[8,6144]{1,0:T(8,128)(2,1)S(1)}, bf16[8,6144]{1,0:T(8,128)(2,1)S(1)}, u32[]{:S(2)}, u32[]{:S(2)}) collective-permute-start(bf16[8,6144]{1,0:T(8,128)(2,1)S(1)} %get-tuple-element.39), channel_id=1, source_target_pairs={{0,6},{1,7},{2,4},{3,5},{4,2},{5,3},{6,0},{7,1},{8,14},{9,15},{10,... | collective-permute-start | bytes 294920 | tf_op jit(solution)/shard_map/ppermute | solution.py:422
  10.5 12.5 %collective-permute-start.11 = (bf16[16,6144]{1,0:T(8,128)(2,1)S(1)}, bf16[16,6144]{1,0:T(8,128)(2,1)S(1)}, u32[]{:S(2)}, u32[]{:S(2)}) collective-permute-start(bf16[16,6144]{1,0:T(8,128)(2,1)S(1)} %get-tuple-element.46), channel_id=1, source_target_pairs={{0,1},{1,2},{2,3},{3,4},{4,5},{5,6},{6,7},{7,0},{8,9},{9,10},{10,1... | collective-permute-start | bytes 589832 | tf_op jit(solution)/shard_map/ppermute | solution.py:422
  18.4 6.6 %collective-permute-start.6 = (bf16[8,6144]{1,0:T(8,128)(2,1)S(1)}, bf16[8,6144]{1,0:T(8,128)(2,1)S(1)}, u32[]{:S(2)}, u32[]{:S(2)}) collective-permute-start(bf16[8,6144]{1,0:T(8,128)(2,1)S(1)} %get-tuple-element.45.refs_0_), channel_id=1, source_target_pairs={{0,6},{1,7},{2,4},{3,5},{4,2},{5,3},{6,0},{7,1},{8,14},{9,15},{10,... | collective-permute-start | bytes 294920 | tf_op jit(solution)/shard_map/ppermute | solution.py:422
  21.0 5.3 %collective-permute-start.5 = (bf16[8,6144]{1,0:T(8,128)(2,1)S(1)}, bf16[8,6144]{1,0:T(8,128)(2,1)S(1)}, u32[]{:S(2)}, u32[]{:S(2)}) collective-permute-start(bf16[8,6144]{1,0:T(8,128)(2,1)S(1)} %get-tuple-element.45.refs_0_), channel_id=1, source_target_pairs={{0,2},{1,3},{2,0},{3,1},{4,6},{5,7},{6,4},{7,5},{8,10},{9,11},{10,... | collective-permute-start | bytes 294920 | tf_op jit(solution)/shard_map/ppermute | solution.py:422
  22.8 9.4 %collective-permute-start.4 = (bf16[8,6144]{1,0:T(8,128)(2,1)S(1)}, bf16[8,6144]{1,0:T(8,128)(2,1)S(1)}, u32[]{:S(2)}, u32[]{:S(2)}) collective-permute-start(bf16[8,6144]{1,0:T(8,128)(2,1)S(1)} %get-tuple-element.45.refs_0_), channel_id=1, source_target_pairs={{0,4},{1,5},{2,6},{3,7},{4,0},{5,1},{6,2},{7,3},{8,12},{9,13},{10,... | collective-permute-start | bytes 294920 | tf_op jit(solution)/shard_map/ppermute | solution.py:422
  23.0 12.9 %collective-permute-start.7 = (bf16[8,6144]{1,0:T(8,128)(2,1)S(1)}, bf16[8,6144]{1,0:T(8,128)(2,1)S(1)}, u32[]{:S(2)}, u32[]{:S(2)}) collective-permute-start(bf16[8,6144]{1,0:T(8,128)(2,1)S(1)} %get-tuple-element.45.refs_0_), channel_id=1, source_target_pairs={{0,1},{1,0},{2,3},{3,2},{4,5},{5,4},{6,7},{7,6},{8,9},{9,8},{10,11... | collective-permute-start | bytes 294920 | tf_op jit(solution)/shard_map/ppermute | solution.py:422
  23.0 12.9 %collective-permute-start.12 = (bf16[8,6144]{1,0:T(8,128)(2,1)S(1)}, bf16[8,6144]{1,0:T(8,128)(2,1)S(1)}, u32[]{:S(2)}, u32[]{:S(2)}) collective-permute-start(bf16[8,6144]{1,0:T(8,128)(2,1)S(1)} %get-tuple-element.47), channel_id=1, source_target_pairs={{0,1},{1,2},{2,3},{3,4},{4,5},{5,6},{6,7},{7,0},{8,9},{9,10},{10,1... | collective-permute-start | bytes 294920 | tf_op jit(solution)/shard_map/ppermute | solution.py:422
  25.0 10.9 %collective-permute-start.10 = (bf16[8,6144]{1,0:T(8,128)(2,1)S(1)}, bf16[8,6144]{1,0:T(8,128)(2,1)S(1)}, u32[]{:S(2)}, u32[]{:S(2)}) collective-permute-start(bf16[8,6144]{1,0:T(8,128)(2,1)S(1)} %collective-permute-done.6.refs_3_), channel_id=1, source_target_pairs={{0,1},{1,0},{2,3},{3,2},{4,5},{5,4},{6,7},{7,6},{8,9},{9,8},{10,11... | collective-permute-start | bytes 294920 | tf_op jit(solution)/shard_map/ppermute | solution.py:422
  26.3 9.7 %collective-permute-start.9 = (bf16[8,6144]{1,0:T(8,128)(2,1)S(1)}, bf16[8,6144]{1,0:T(8,128)(2,1)S(1)}, u32[]{:S(2)}, u32[]{:S(2)}) collective-permute-start(bf16[8,6144]{1,0:T(8,128)(2,1)S(1)} %collective-permute-done.5.refs_2_), channel_id=1, source_target_pairs={{0,1},{1,0},{2,3},{3,2},{4,5},{5,4},{6,7},{7,6},{8,9},{9,8},{10,11... | collective-permute-start | bytes 294920 | tf_op jit(solution)/shard_map/ppermute | solution.py:422
  32.1 3.8 %collective-permute-start.8 = (bf16[8,6144]{1,0:T(8,128)(2,1)S(1)}, bf16[8,6144]{1,0:T(8,128)(2,1)S(1)}, u32[]{:S(2)}, u32[]{:S(2)}) collective-permute-start(bf16[8,6144]{1,0:T(8,128)(2,1)S(1)} %collective-permute-done.4.refs_1_), channel_id=1, source_target_pairs={{0,1},{1,0},{2,3},{3,2},{4,5},{5,4},{6,7},{7,6},{8,9},{9,8},{10,11... | collective-permute-start | bytes 294920 | tf_op jit(solution)/shard_map/ppermute | solution.py:422

commit v3 on v2

--- a/solution.py
+++ b/solution.py
@@ -359,18 +359,49 @@
     )(fix, *states, grads)
 
 
-def place_kernel(chips, table, *refs):
-    near, far = refs[:chips], refs[chips : 2 * chips]
-    packed, moved, weights, checkpoint, partner, sems = refs[2 * chips :]
+def placing(places, chips, table, near, far, weights, sems):
+    block = near[0].shape[0]
+    rows = table[...]
+    copies = []
+    for at, *pieces in zip(places, near, far):
+        for sibling, piece in enumerate(pieces):
+            row = pl.multiple_of(rows[at + sibling * chips, 0], block)
+            target = weights.at[pl.ds(row, block), :]
+            copies.append(pltpu.make_async_copy(piece, target, sems.at[len(copies)]))
+    return copies
+
+
+def early_kernel(chips, table, *refs):
+    count = chips - 1
+    copies = placing(range(count), chips, table, refs[:count], refs[count : 2 * count], *refs[-2:])
+    for copy in copies:
+        copy.start()
+    for copy in copies:
+        copy.wait()
+
+
+def place_early(table, near, far):
+    block, width = near[0].shape
+    chips = len(near) + 1
+    return pl.pallas_call(
+        functools.partial(early_kernel, chips),
+        in_specs=[VMEM()] * (2 * chips - 1),
+        out_specs=HBM(),
+        out_shape=jax.ShapeDtypeStruct((2 * chips * block, width), jnp.bfloat16),
+        scratch_shapes=[pltpu.SemaphoreType.DMA((2 * chips - 2,))],
+        compiler_params=params(),
+        cost_estimate=cost(0, 8 * chips * block * width),
+        name="place_early",
+    )(table, *near, *far)
+
+
+def late_kernel(chips, table, near, *refs):
+    far, (packed, moved, _, weights, checkpoint, partner, sems) = refs[:chips], refs[chips:]
     block = moved.shape[0]
     replicas = 2 * chips
     me = lax.axis_index("replica")
     previous = lax.rem(me + replicas - 1, replicas)
-    rows = table[...]
-    copies = []
-    for at, piece in enumerate((*near, *far)):
-        target = weights.at[pl.ds(pl.multiple_of(rows[at, 0], block), block), :]
-        copies.append(pltpu.make_async_copy(piece, target, sems.at[at]))
+    copies = placing([chips - 1], chips, table, [near], far[-1:], weights, sems)
     for copy in copies:
         copy.start()
     grads = moved[...].astype(jnp.float32)
@@ -382,33 +413,33 @@
         def _():
             partner[0] = piece[...].astype(jnp.float32)
 
-    last = pltpu.make_async_copy(partner, checkpoint, sems.at[replicas])
+    last = pltpu.make_async_copy(partner, checkpoint, sems.at[2])
     last.start()
     for copy in copies:
         copy.wait()
     last.wait()
 
 
-def place(table, near, far, packed, moved):
+def place_late(table, near, far, packed, moved, weights):
     block, width = moved.shape
-    chips = len(near)
-    rows = 2 * chips * block
-    return pl.pallas_call(
-        functools.partial(place_kernel, chips),
-        in_specs=[VMEM()] * (2 * chips + 3),
+    chips = len(far)
+    return pl.pallas_call(
+        functools.partial(late_kernel, chips),
+        in_specs=[VMEM()] * (chips + 4) + [HBM()],
         out_specs=[HBM()] * 2,
         out_shape=[
-            jax.ShapeDtypeStruct((rows, width), jnp.bfloat16),
+            jax.ShapeDtypeStruct(weights.shape, weights.dtype),
             jax.ShapeDtypeStruct((3, block, width), jnp.float32),
         ],
+        input_output_aliases={chips + 4: 0},
         scratch_shapes=[
             pltpu.VMEM((3, block, width), jnp.float32),
-            pltpu.SemaphoreType.DMA((2 * chips + 1,)),
-        ],
-        compiler_params=params(),
-        cost_estimate=cost(0, 8 * rows * width),
-        name="place",
-    )(table, *near, *far, packed, moved)
+            pltpu.SemaphoreType.DMA((3,)),
+        ],
+        compiler_params=params(),
+        cost_estimate=cost(0, 20 * block * width),
+        name="place_late",
+    )(table, near, *far, packed, moved, weights)
 
 
 def tiled_device(
@@ -450,7 +481,8 @@
     updated = new_states(fix, states, grads)
     moved = along_ring(send_grads)
     far = [to_sibling(piece) for piece in near]
-    weights_new, checkpoint = place(table, near, far, packed, moved)
+    weights_new = place_early(table, near[:-1], far[:-1])
+    weights_new, checkpoint = place_late(table, near[-1], far, packed, moved, weights_new)
     return (*updated, checkpoint, weights_new, hidden_grad.T[None])
 
 

time: 37.7 us -> 38.7 us (1.027)
  the two profiles are of different devices: /device:TPU:0 before, /device:TPU:9 now
where the time goes in v3:
time: 38.7 us; the launch traced here: 38.5 us
  waiting for transfers between devices  15.3 us (40%)
  starting transfers between devices  12.7 us (33%)
  Pallas kernels  9.18 us (24%)
  between operations  1.4 us (4%)
    ppermute x13, waiting for transfers between devices, permuted(): lax.ppermute(piece, 'replica', [(i, target(i)) for i in range(replicas)])  15.3 us
    ppermute x13, starting transfers between devices, permuted(): lax.ppermute(piece, 'replica', [(i, target(i)) for i in range(replicas)])  12.7 us
    pallas_call x2, Pallas kernels, hidden_gradient(): pl.pallas_call(functools.partial(back_kernel, width ** (-0.5), core), in_...  2.87 us
    pallas_call x1, Pallas kernels, slab_to_send(): pl.pallas_call(send_kernel, in_specs=[HBM()] * 5, out_specs=[VMEM()] * 7,...  2.25 us
    pallas_call x1, Pallas kernels, place_late(): pl.pallas_call(functools.partial(late_kernel, chips), in_specs=[VMEM()] *...  0.98 us
    pallas_call x1, Pallas kernels, slab_to_keep(): pl.pallas_call(keep_kernel, in_specs=[VMEM()] * 2 + [HBM()], out_specs=[V...  0.93 us
    pallas_call x1, Pallas kernels, new_states(): pl.pallas_call(states_kernel, in_specs=[VMEM()] * 5, out_specs=[VMEM()] *...  0.9 us
    pallas_call x1, Pallas kernels, place_early(): pl.pallas_call(functools.partial(early_kernel, chips), in_specs=[VMEM()]...  0.89 us
  transfers between devices with their start and end apart: 13, of which 6 were waited for; matrix products, arithmetic and copies ran while one was open for 0% of the time, Pallas kernels for 15%

profile of v3, /device:TPU:9, one launch (start us, length us, event | category | flops | bytes accessed | tf_op | source)
XLA Modules:
  0.0 38.5 jit_solution(17623603563956005467)
XLA Ops:
  0.6 2.2 %slab_to_send.1 = (bf16[32,6144]{1,0:T(8,128)(2,1)S(1)}, bf16[256,6144]{1,0:T(8,128)(2,1)S(1)}, bf16[32,256]{1,0:T(8,128)(2,1)S(1)}, f32[8,6144]{1,0:T(8,128)S(1...) custom-call(s32[8]{0:T(128)} %order_hbm.1, bf16[64,256]{1,0:T(8,128)(2,1)} %bitcast.9, ...), custom_call_target="tpu_custom_call" | custom-call | flops 100663296 | bytes 3145728 | tf_op jit(solution)/shard_map/slab_to_send/pallas_call | solution.py:167
  2.9 0.7 %collective-permute-start = (bf16[32,6144]{1,0:T(8,128)(2,1)S(1)}, bf16[32,6144]{1,0:T(8,128)(2,1)S(1)}, u32[]{:S(2)}, u32[]{:S(2)}) collective-permute-start(bf16[32,6144]{1,0:T(8,128)(2,1)S(1)} %get-tuple-element.31), channel_id=1, source_target_pairs={{0,1},{1,0},{2,3},{3,2},{4,5},{5,4},{6,7},{7,6},{8,9},{9,8},{10,11... | collective-permute-start | bytes 1179656 | tf_op jit(solution)/shard_map/ppermute | solution.py:453
  3.6 0.9 %slab_to_keep.1 = (f32[32,6144]{1,0:T(8,128)S(1)}, f32[8,6144]{1,0:T(8,128)S(1)}) custom-call(bf16[32,256]{1,0:T(8,128)(2,1)S(1)} %get-tuple-element.28.picked, bf16[256,6144]{1,0:T(8,128)(2,1)S(1)} %get-tuple-element.29.grads, f32[8,6144]{1,0:T(8,128)} %master_hbm.1), custom_call_target="tpu_custom_call" | custom-call | flops 100663296 | bytes 3145728 | tf_op jit(solution)/shard_map/slab_to_keep/pallas_call | solution.py:206
  4.6 0.4 %collective-permute-done.got_ref = bf16[32,6144]{1,0:T(8,128)(2,1)S(1)} collective-permute-done((bf16[32,6144]{1,0:T(8,128)(2,1)S(1)}, bf16[32,6144]{1,0:T(8,128)(2,1)S(1)}, u32[]{:S(2)}, u32[]{:S(2)}) %collective-permute-start) | collective-permute-done | bytes 393248 | tf_op jit(solution)/shard_map/ppermute | solution.py:453
  5.0 0.1 pair_sum.1
  5.0 0.1 collective-permute-start.1
  5.1 2.5 %collective-permute-start.2 = (bf16[8,6144]{1,0:T(8,128)(2,1)S(1)}, bf16[8,6144]{1,0:T(8,128)(2,1)S(1)}, u32[]{:S(2)}, u32[]{:S(2)}) collective-permute-start(bf16[8,6144]{1,0:T(8,128)(2,1)S(1)} %get-tuple-element.38), channel_id=1, source_target_pairs={{0,2},{1,5},{2,0},{3,7},{4,6},{5,1},{6,4},{7,3},{8,10},{9,13},{10,... | collective-permute-start | bytes 294920 | tf_op jit(solution)/shard_map/ppermute | solution.py:453
  7.6 0.2 collective-permute-start.3
  8.4 0.2 collective-permute-done.1.refs_1_
  8.6 3.5 %collective-permute-done.2.refs_2_ = bf16[8,6144]{1,0:T(8,128)(2,1)S(1)} collective-permute-done((bf16[8,6144]{1,0:T(8,128)(2,1)S(1)}, bf16[8,6144]{1,0:T(8,128)(2,1)S(1)}, u32[]{:S(2)}, u32[]{:S(2)}) %collective-permute-start.2) | collective-permute-done | bytes 98336 | tf_op jit(solution)/shard_map/ppermute | solution.py:453
  12.1 4.3 %collective-permute-done.3.refs_3_ = bf16[8,6144]{1,0:T(8,128)(2,1)S(1)} collective-permute-done((bf16[8,6144]{1,0:T(8,128)(2,1)S(1)}, bf16[8,6144]{1,0:T(8,128)(2,1)S(1)}, u32[]{:S(2)}, u32[]{:S(2)}) %collective-permute-start.3) | collective-permute-done | bytes 98336 | tf_op jit(solution)/shard_map/ppermute | solution.py:453
  16.3 0.3 update.1
  16.6 0.1 collective-permute-start.8
  16.7 2.9 %collective-permute-start.6 = (bf16[8,6144]{1,0:T(8,128)(2,1)S(1)}, bf16[8,6144]{1,0:T(8,128)(2,1)S(1)}, u32[]{:S(2)}, u32[]{:S(2)}) collective-permute-start(bf16[8,6144]{1,0:T(8,128)(2,1)S(1)} %get-tuple-element.45.refs_0_), channel_id=1, source_target_pairs={{0,4},{1,5},{2,6},{3,7},{4,0},{5,1},{6,2},{7,3},{8,12},{9,13},{10,... | collective-permute-start | bytes 294920 | tf_op jit(solution)/shard_map/ppermute | solution.py:453
  19.6 1.6 %collective-permute-start.5 = (bf16[8,6144]{1,0:T(8,128)(2,1)S(1)}, bf16[8,6144]{1,0:T(8,128)(2,1)S(1)}, u32[]{:S(2)}, u32[]{:S(2)}) collective-permute-start(bf16[8,6144]{1,0:T(8,128)(2,1)S(1)} %get-tuple-element.45.refs_0_), channel_id=1, source_target_pairs={{0,1},{1,0},{2,3},{3,2},{4,5},{5,4},{6,7},{7,6},{8,9},{9,8},{10,11... | collective-permute-start | bytes 294920 | tf_op jit(solution)/shard_map/ppermute | solution.py:453
  21.2 0.0 collective-permute-start.11
  21.2 0.0 collective-permute-start.4
  21.2 0.0 collective-permute-done.8.refs_2_
  21.2 1.3 %collective-permute-start.9 = (bf16[8,6144]{1,0:T(8,128)(2,1)S(1)}, bf16[8,6144]{1,0:T(8,128)(2,1)S(1)}, u32[]{:S(2)}, u32[]{:S(2)}) collective-permute-start(bf16[8,6144]{1,0:T(8,128)(2,1)S(1)} %collective-permute-done.8.refs_2_), channel_id=1, source_target_pairs={{0,1},{1,0},{2,3},{3,2},{4,5},{5,4},{6,7},{7,6},{8,9},{9,8},{10,11... | collective-permute-start | bytes 294920 | tf_op jit(solution)/shard_map/ppermute | solution.py:453
  22.5 1.1 %collective-permute-done.6.refs_1_ = bf16[8,6144]{1,0:T(8,128)(2,1)S(1)} collective-permute-done((bf16[8,6144]{1,0:T(8,128)(2,1)S(1)}, bf16[8,6144]{1,0:T(8,128)(2,1)S(1)}, u32[]{:S(2)}, u32[]{:S(2)}) %collective-permute-start.6) | collective-permute-done | bytes 98336 | tf_op jit(solution)/shard_map/ppermute | solution.py:453
  23.5 2.9 %collective-permute-start.7 = (bf16[8,6144]{1,0:T(8,128)(2,1)S(1)}, bf16[8,6144]{1,0:T(8,128)(2,1)S(1)}, u32[]{:S(2)}, u32[]{:S(2)}) collective-permute-start(bf16[8,6144]{1,0:T(8,128)(2,1)S(1)} %collective-permute-done.6.refs_1_), channel_id=1, source_target_pairs={{0,1},{1,0},{2,3},{3,2},{4,5},{5,4},{6,7},{7,6},{8,9},{9,8},{10,11... | collective-permute-start | bytes 294920 | tf_op jit(solution)/shard_map/ppermute | solution.py:453
  26.4 0.0 collective-permute-done.5.refs_3_.refs_0_
  26.4 0.0 collective-permute-start.12
  26.4 5.9 %collective-permute-done.4.near = bf16[8,6144]{1,0:T(8,128)(2,1)S(1)} collective-permute-done((bf16[8,6144]{1,0:T(8,128)(2,1)S(1)}, bf16[8,6144]{1,0:T(8,128)(2,1)S(1)}, u32[]{:S(2)}, u32[]{:S(2)}) %collective-permute-start.4) | collective-permute-done | bytes 98336 | tf_op jit(solution)/shard_map/ppermute | solution.py:453
  32.3 0.5 %collective-permute-start.10 = (bf16[8,6144]{1,0:T(8,128)(2,1)S(1)}, bf16[8,6144]{1,0:T(8,128)(2,1)S(1)}, u32[]{:S(2)}, u32[]{:S(2)}) collective-permute-start(bf16[8,6144]{1,0:T(8,128)(2,1)S(1)} %collective-permute-done.4.near), channel_id=1, source_target_pairs={{0,1},{1,0},{2,3},{3,2},{4,5},{5,4},{6,7},{7,6},{8,9},{9,8},{10,11... | collective-permute-start | bytes 294920 | tf_op jit(solution)/shard_map/ppermute | solution.py:453
  32.8 2.8 %hidden_gradient.2.refs_0_ = bf16[64,256]{1,0:T(8,128)(2,1)} custom-call(bf16[64,6144]{1,0:T(8,128)(2,1)} %weights_hbm.3, bf16[256,6144]{1,0:T(8,128)(2,1)S(1)} %get-tuple-element.29.grads), custom_call_target="tpu_custom_call" | custom-call | flops 201326592 | bytes 3932160 | tf_op jit(solution)/shard_map/hidden_gradient/pallas_call | solution.py:252
  35.7 0.9 %new_states.1 = (f32[8,6144]{1,0:T(8,128)}, f32[8,6144]{1,0:T(8,128)}, f32[8,6144]{1,0:T(8,128)}) custom-call(f32[16,128]{1,0:T(8,128)S(1)} %corrections.1.fix, f32[8,6144]{1,0:T(8,128)S(1)} %get-tuple-element.34.refs_4_.master, f32[8,6144]{1,0:T(8,128)S(1)} %get-tuple-element.35.refs_5_.first, f32[8,6144]{1,0:T(8,128)S(1)} %get-tuple-element.36.refs_6_.second, ...), custom_call_target="tpu_custom_call" | custom-call | flops 983040 | bytes 1376256 | tf_op jit(solution)/shard_map/new_states/pallas_call | solution.py:351
  36.6 0.0 collective-permute-done.9.refs_5_.refs_2_
  36.6 0.0 collective-permute-done.7.refs_4_.refs_1_
  36.6 0.9 %place_early.1.refs_6_ = bf16[64,6144]{1,0:T(8,128)(2,1)} custom-call(s32[8,128]{1,0:T(8,128)S(1)} %get-tuple-element.44.table, bf16[8,6144]{1,0:T(8,128)(2,1)S(1)} %get-tuple-element.45.refs_0_, bf16[8,6144]{1,0:T(8,128)(2,1)S(1)} %collective-permute-done.6.refs_1_, bf16[8,6144]{1,0:T(8,128)(2,1)S(1)} %collective-permute-done.8.refs_2_, ...), custom_call_target="tpu_custom_call" | custom-call | bytes 1572864 | tf_op jit(solution)/shard_map/place_early/pallas_call | solution.py:386
  37.5 0.0 collective-permute-done.11.refs_4_
  37.5 0.0 collective-permute-done.12.refs_5_
  37.5 0.0 collective-permute-done.10.refs_3_
  37.6 1.0 %place_late.1 = (bf16[64,6144]{1,0:T(8,128)(2,1)}, f32[3,8,6144]{2,1,0:T(8,128)}) custom-call(s32[8,128]{1,0:T(8,128)S(1)} %get-tuple-element.44.table, bf16[8,6144]{1,0:T(8,128)(2,1)S(1)} %collective-permute-done.4.near, bf16[8,6144]{1,0:T(8,128)(2,1)S(1)} %collective-permute-done.5.refs_3_.refs_0_, ...), custom_call_target="tpu_custom_call", output_to_operand_aliasing={{0}: (8, {})} | custom-call | bytes 983040 | tf_op jit(solution)/shard_map/place_late/pallas_call | solution.py:426
  (2 shorter events, 0.1 us)
Async XLA Ops:
  2.9 2.1 %collective-permute-start = (bf16[32,6144]{1,0:T(8,128)(2,1)S(1)}, bf16[32,6144]{1,0:T(8,128)(2,1)S(1)}, u32[]{:S(2)}, u32[]{:S(2)}) collective-permute-start(bf16[32,6144]{1,0:T(8,128)(2,1)S(1)} %get-tuple-element.31), channel_id=1, source_target_pairs={{0,1},{1,0},{2,3},{3,2},{4,5},{5,4},{6,7},{7,6},{8,9},{9,8},{10,11... | collective-permute-start | bytes 1179656 | tf_op jit(solution)/shard_map/ppermute | solution.py:453
  5.0 3.5 %collective-permute-start.1 = (bf16[8,6144]{1,0:T(8,128)(2,1)S(1)}, bf16[8,6144]{1,0:T(8,128)(2,1)S(1)}, u32[]{:S(2)}, u32[]{:S(2)}) collective-permute-start(bf16[8,6144]{1,0:T(8,128)(2,1)S(1)} %get-tuple-element.37), channel_id=1, source_target_pairs={{0,4},{1,3},{2,6},{3,1},{4,0},{5,7},{6,2},{7,5},{8,12},{9,11},{10,... | collective-permute-start | bytes 294920 | tf_op jit(solution)/shard_map/ppermute | solution.py:453
  5.1 6.9 %collective-permute-start.2 = (bf16[8,6144]{1,0:T(8,128)(2,1)S(1)}, bf16[8,6144]{1,0:T(8,128)(2,1)S(1)}, u32[]{:S(2)}, u32[]{:S(2)}) collective-permute-start(bf16[8,6144]{1,0:T(8,128)(2,1)S(1)} %get-tuple-element.38), channel_id=1, source_target_pairs={{0,2},{1,5},{2,0},{3,7},{4,6},{5,1},{6,4},{7,3},{8,10},{9,13},{10,... | collective-permute-start | bytes 294920 | tf_op jit(solution)/shard_map/ppermute | solution.py:453
  7.6 8.8 %collective-permute-start.3 = (bf16[8,6144]{1,0:T(8,128)(2,1)S(1)}, bf16[8,6144]{1,0:T(8,128)(2,1)S(1)}, u32[]{:S(2)}, u32[]{:S(2)}) collective-permute-start(bf16[8,6144]{1,0:T(8,128)(2,1)S(1)} %get-tuple-element.39), channel_id=1, source_target_pairs={{0,6},{1,7},{2,4},{3,5},{4,2},{5,3},{6,0},{7,1},{8,14},{9,15},{10,... | collective-permute-start | bytes 294920 | tf_op jit(solution)/shard_map/ppermute | solution.py:453
  16.6 4.6 %collective-permute-start.8 = (bf16[8,6144]{1,0:T(8,128)(2,1)S(1)}, bf16[8,6144]{1,0:T(8,128)(2,1)S(1)}, u32[]{:S(2)}, u32[]{:S(2)}) collective-permute-start(bf16[8,6144]{1,0:T(8,128)(2,1)S(1)} %get-tuple-element.45.refs_0_), channel_id=1, source_target_pairs={{0,2},{1,3},{2,0},{3,1},{4,6},{5,7},{6,4},{7,5},{8,10},{9,11},{10,... | collective-permute-start | bytes 294920 | tf_op jit(solution)/shard_map/ppermute | solution.py:453
  16.7 6.8 %collective-permute-start.6 = (bf16[8,6144]{1,0:T(8,128)(2,1)S(1)}, bf16[8,6144]{1,0:T(8,128)(2,1)S(1)}, u32[]{:S(2)}, u32[]{:S(2)}) collective-permute-start(bf16[8,6144]{1,0:T(8,128)(2,1)S(1)} %get-tuple-element.45.refs_0_), channel_id=1, source_target_pairs={{0,4},{1,5},{2,6},{3,7},{4,0},{5,1},{6,2},{7,3},{8,12},{9,13},{10,... | collective-permute-start | bytes 294920 | tf_op jit(solution)/shard_map/ppermute | solution.py:453
  19.6 6.8 %collective-permute-start.5 = (bf16[8,6144]{1,0:T(8,128)(2,1)S(1)}, bf16[8,6144]{1,0:T(8,128)(2,1)S(1)}, u32[]{:S(2)}, u32[]{:S(2)}) collective-permute-start(bf16[8,6144]{1,0:T(8,128)(2,1)S(1)} %get-tuple-element.45.refs_0_), channel_id=1, source_target_pairs={{0,1},{1,0},{2,3},{3,2},{4,5},{5,4},{6,7},{7,6},{8,9},{9,8},{10,11... | collective-permute-start | bytes 294920 | tf_op jit(solution)/shard_map/ppermute | solution.py:453
  21.2 16.3 %collective-permute-start.11 = (bf16[16,6144]{1,0:T(8,128)(2,1)S(1)}, bf16[16,6144]{1,0:T(8,128)(2,1)S(1)}, u32[]{:S(2)}, u32[]{:S(2)}) collective-permute-start(bf16[16,6144]{1,0:T(8,128)(2,1)S(1)} %get-tuple-element.46), channel_id=1, source_target_pairs={{0,1},{1,2},{2,3},{3,4},{4,5},{5,6},{6,7},{7,0},{8,9},{9,10},{10,1... | collective-permute-start | bytes 589832 | tf_op jit(solution)/shard_map/ppermute | solution.py:453
  21.2 11.1 %collective-permute-start.4 = (bf16[8,6144]{1,0:T(8,128)(2,1)S(1)}, bf16[8,6144]{1,0:T(8,128)(2,1)S(1)}, u32[]{:S(2)}, u32[]{:S(2)}) collective-permute-start(bf16[8,6144]{1,0:T(8,128)(2,1)S(1)} %get-tuple-element.45.refs_0_), channel_id=1, source_target_pairs={{0,6},{1,7},{2,4},{3,5},{4,2},{5,3},{6,0},{7,1},{8,14},{9,15},{10,... | collective-permute-start | bytes 294920 | tf_op jit(solution)/shard_map/ppermute | solution.py:453
  21.2 15.4 %collective-permute-start.9 = (bf16[8,6144]{1,0:T(8,128)(2,1)S(1)}, bf16[8,6144]{1,0:T(8,128)(2,1)S(1)}, u32[]{:S(2)}, u32[]{:S(2)}) collective-permute-start(bf16[8,6144]{1,0:T(8,128)(2,1)S(1)} %collective-permute-done.8.refs_2_), channel_id=1, source_target_pairs={{0,1},{1,0},{2,3},{3,2},{4,5},{5,4},{6,7},{7,6},{8,9},{9,8},{10,11... | collective-permute-start | bytes 294920 | tf_op jit(solution)/shard_map/ppermute | solution.py:453
  23.5 13.1 %collective-permute-start.7 = (bf16[8,6144]{1,0:T(8,128)(2,1)S(1)}, bf16[8,6144]{1,0:T(8,128)(2,1)S(1)}, u32[]{:S(2)}, u32[]{:S(2)}) collective-permute-start(bf16[8,6144]{1,0:T(8,128)(2,1)S(1)} %collective-permute-done.6.refs_1_), channel_id=1, source_target_pairs={{0,1},{1,0},{2,3},{3,2},{4,5},{5,4},{6,7},{7,6},{8,9},{9,8},{10,11... | collective-permute-start | bytes 294920 | tf_op jit(solution)/shard_map/ppermute | solution.py:453
  26.4 11.1 %collective-permute-start.12 = (bf16[8,6144]{1,0:T(8,128)(2,1)S(1)}, bf16[8,6144]{1,0:T(8,128)(2,1)S(1)}, u32[]{:S(2)}, u32[]{:S(2)}) collective-permute-start(bf16[8,6144]{1,0:T(8,128)(2,1)S(1)} %get-tuple-element.47), channel_id=1, source_target_pairs={{0,1},{1,2},{2,3},{3,4},{4,5},{5,6},{6,7},{7,0},{8,9},{9,10},{10,1... | collective-permute-start | bytes 294920 | tf_op jit(solution)/shard_map/ppermute | solution.py:453
  32.3 5.2 %collective-permute-start.10 = (bf16[8,6144]{1,0:T(8,128)(2,1)S(1)}, bf16[8,6144]{1,0:T(8,128)(2,1)S(1)}, u32[]{:S(2)}, u32[]{:S(2)}) collective-permute-start(bf16[8,6144]{1,0:T(8,128)(2,1)S(1)} %collective-permute-done.4.near), channel_id=1, source_target_pairs={{0,1},{1,0},{2,3},{3,2},{4,5},{5,4},{6,7},{7,6},{8,9},{9,8},{10,11... | collective-permute-start | bytes 294920 | tf_op jit(solution)/shard_map/ppermute | solution.py:453
